TPU v7x, 32 devices: a whole 2x2x4 slice. The times are simulated.
32 devices in a mesh: groups: 2 (over x), space: 16 (over z, y, core).
Axes of the slice: x: 2, y: 2, z: 4, core: 2. Of those that a mesh axis runs over, the one named last changes fastest.
Arguments:
- noisy: bfloat16 [16384, 512], P(('groups', 'space')), parts along dimension 0, may hold values from -6 to 6
- matches: int32 [3072, 16], P(('groups', 'space')), parts along dimension 0, may hold values from 0 to 8191, as said below
- cube_home: int32 [16384], P('groups'), parts along dimension 0, may hold values from 0 to 8191, as said below
- sigma_coef: float32 [512], replicated, may hold values from 0.3 to 1.5
Outputs:
- basic: bfloat16 [16384, 512], P(('groups', 'space')), parts along dimension 0
- final: bfloat16 [16384, 512], P(('groups', 'space')), parts along dimension 0
There are 2 independent parts, one for each index of `groups`. A program takes and returns all parts, laid end to end along the dimension named above; an argument that names none is the same for every part. Nothing has to cross between parts.
Inputs may be any that keep to these rules, and one draw needn't show every extreme that they name: `matches`: each device's 16 * 96 list entries name at most 192 cubes whose table rows lie in any one device's block of 512 rows; in every draw one block receives exactly 192 from every device. `cube_home`: A permutation of the table rows.
All inputs are finite; a program needn't handle non-finite values.
Results may differ from a plain program's by a relative error of at most 0.0079.
Values may be sent and summed in bfloat16 or wider, within the bound.
A program may use at most 64 MiB of HBM per device.

v0:
```python
import functools

import jax
import jax.numpy as jnp
import numpy as np
from jax import lax
from jax.experimental import pallas as pl
from jax.experimental.pallas import tpu as pltpu
from jax.sharding import PartitionSpec as P

shrink_level = 2.7
prior_weight = 0.5
LANES = 128
CHUNK = 512
ROWS = 384
TOGETHER = 2
LAG = 3


def dct_matrix(length):
    index = np.arange(length, dtype=np.float64)
    table = np.cos(np.pi * (2.0 * index[None, :] + 1.0) * index[:, None] / (2.0 * length))
    table = table * np.sqrt(2.0 / length)
    table[0] /= np.sqrt(2.0)
    return table


def split(value):
    high = value.astype(jnp.bfloat16)
    return high, (value - high.astype(jnp.float32)).astype(jnp.bfloat16)


def make_tables(group):
    small = dct_matrix(8)
    cube = np.kron(np.kron(small, small), small).astype(np.float32)
    mix = np.kron(np.eye(LANES // group), dct_matrix(group)).astype(np.float32)
    mixes = [
        np.concatenate([np.asarray(half, np.float32) for half in split(each)], axis=1)
        for each in (mix, mix.T)
    ]
    return (cube.astype(jnp.bfloat16), cube.T.astype(jnp.bfloat16)) + tuple(
        each.astype(jnp.bfloat16) for each in mixes
    )


def mix_rows(table, value):
    both, high = table, table[:, :LANES]
    pieces = []
    for i in range(0, value.shape[0], LANES):
        top, low = split(value[i : i + LANES])
        pieces.append(
            jnp.dot(both, jnp.concatenate([top, top], axis=0), preferred_element_type=jnp.float32)
            + jnp.dot(high, low, preferred_element_type=jnp.float32)
        )
    return jnp.concatenate(pieces, axis=0)


def kernel(second, group, *refs):
    rows_in, sigma, cube, cube_t, mix, mix_t, taken_in, coeffs, acc_out, wsum = refs[:10]
    big, members, stage, sem = refs[-4:]
    cubes, width = acc_out.shape
    full = big.shape[1]
    groups = members.shape[0]
    entries = groups * group
    chunks = cubes // CHUNK
    steps = entries // ROWS

    noise = sigma[...] * sigma[...]
    level = (shrink_level * sigma[...]) * (shrink_level * sigma[...])

    def compute_step(b, carry):
        rows = pl.ds(pl.multiple_of(b * ROWS, ROWS), ROWS)
        refs_here = ROWS // group
        some = pl.ds(b * refs_here, refs_here)
        cleared = cubes // steps
        big[pl.ds(pl.multiple_of(b * cleared, cleared), cleared), :] = jnp.zeros(
            (cleared, full), jnp.float32
        )
        spec = jnp.dot(taken_in[rows, :], cube_t[...], preferred_element_type=jnp.float32)
        own = mix_rows(mix[...], spec)
        square = own * own
        if second:
            gain = square / (square + noise)
            energy = gain * gain * noise
            shrunk = gain * coeffs[rows, :]
        else:
            coeffs[rows, :] = own
            gain = square / (square + level)
            energy = gain * gain
            shrunk = gain * own
        total = jnp.sum(jnp.sum(energy, axis=1, keepdims=True).reshape(refs_here, group, 1), axis=1)
        weight = 1.0 / (0.25 + total / (group * width))
        back = mix_rows(mix_t[...], shrunk).astype(jnp.bfloat16)
        out = jnp.dot(back, cube[...], preferred_element_type=jnp.float32)
        each = jnp.broadcast_to(weight[:, None, :], (refs_here, group, 1)).reshape(ROWS, 1)
        part = (each * out).astype(jnp.bfloat16).astype(jnp.float32)
        members[some, :, :width] = part.reshape(refs_here, group, width)
        members[some, :, width:] = jnp.broadcast_to(
            weight[:, None, :].astype(jnp.bfloat16).astype(jnp.float32), (refs_here, group, LANES)
        )
        return carry

    lax.fori_loop(0, steps, compute_step, 0)

    def scatter_step(r, carry):
        base = r * group
        for first in range(0, group, TOGETHER):
            places = [rows_in[base + first + m] for m in range(TOGETHER)]
            added = [members[r, first + m : first + m + 1, :] for m in range(TOGETHER)]
            before = [big[pl.ds(place, 1), :] for place in places]
            for m in range(TOGETHER):
                total = before[m] + added[m]
                for k in range(m):
                    total = total + jnp.where(places[k] == places[m], added[k], 0.0)
                before[m] = total
            for m in range(TOGETHER):
                big[pl.ds(places[m], 1), :] = before[m]
        return carry

    lax.fori_loop(0, groups, scatter_step, 0, unroll=2)

    def put(i, slot):
        rows = pl.ds(pl.multiple_of(i * CHUNK, CHUNK), CHUNK)
        return pltpu.make_async_copy(stage.at[slot], acc_out.at[rows, :], sem.at[slot])

    def store_step(i, carry):
        slot = lax.rem(i, 2)

        @pl.when(i >= 2)
        def _():
            put(i - 2, slot).wait()

        rows = pl.ds(pl.multiple_of(i * CHUNK, CHUNK), CHUNK)
        stage[slot] = big[rows, :width].astype(jnp.bfloat16)
        put(i, slot).start()
        return carry

    lax.fori_loop(0, chunks, store_step, 0)

    lane = lax.broadcasted_iota(jnp.int32, (LANES, LANES), 1)
    sub = lax.broadcasted_iota(jnp.int32, (LANES, LANES), 0)

    def weight_step(i, carry):
        rows = pl.ds(pl.multiple_of(i * LANES, LANES), LANES)
        wsum[pl.ds(i, 1), :] = jnp.sum(
            jnp.where(lane == sub, big[rows, width:], 0.0), axis=0, keepdims=True
        )
        return carry

    lax.fori_loop(0, cubes // LANES, weight_step, 0, unroll=4)
    for i in (chunks - 2, chunks - 1):
        put(i, i % 2).wait()


def phase(second, places, sigma, tables, taken, cubes, group, coeffs=None):
    entries, width = taken.shape
    vmem = pl.BlockSpec(memory_space=pltpu.VMEM)
    smem = pl.BlockSpec(memory_space=pltpu.SMEM)
    held = jax.ShapeDtypeStruct((entries, width), jnp.float32)
    outs = [
        jax.ShapeDtypeStruct((cubes, width), jnp.bfloat16),
        jax.ShapeDtypeStruct((cubes // LANES, LANES), jnp.float32),
    ]
    out_specs = [pl.BlockSpec(memory_space=pltpu.HBM), vmem]
    in_specs = [smem] + [vmem] * 6
    args = [places, sigma, *tables, taken]
    if second:
        in_specs = in_specs + [vmem]
        args = args + [coeffs]
    else:
        outs = [held] + outs
        out_specs = [vmem] + out_specs
    return pl.pallas_call(
        functools.partial(kernel, second, group),
        out_shape=outs,
        in_specs=in_specs,
        out_specs=out_specs,
        scratch_shapes=[
            pltpu.VMEM((cubes, width + LANES), jnp.float32),
            pltpu.VMEM((entries // group, group, width + LANES), jnp.float32),
            pltpu.VMEM((2, CHUNK, width), jnp.bfloat16),
            pltpu.SemaphoreType.DMA((2,)),
        ],
        compiler_params=pltpu.CompilerParams(vmem_limit_bytes=60 * 1024 * 1024),
        name="wiener" if second else "shrink",
    )(*args)


MESH = pl.DeviceIdType.MESH


class Ring:
    def __init__(self, grid, count):
        self.grid, self.chips = grid, count // 2
        self.me = lax.axis_index("space")
        self.core = lax.rem(self.me, 2)
        self.spot = self.spot_of(self.me // 2)
        self.partner = {"space": self.me + 1 - 2 * self.core}
        self.sides = tuple({"space": self.device(sign, self.core)} for sign in (1, -1))

    def spot_of(self, chip):
        if self.grid == 1:
            return chip
        side, along = lax.rem(chip, 2), chip // 2
        return along + side * (self.chips - 1 - 2 * along)

    def chip(self, offset):
        spot = lax.rem(self.spot + offset + self.chips, self.chips)
        if self.grid == 1:
            return spot
        side = (2 * spot) // self.chips
        return (spot + side * (self.chips - 1 - 2 * spot)) * 2 + side

    def device(self, offset, core):
        return self.chip(offset) * 2 + core

    def greet(self):
        barrier = pltpu.get_barrier_semaphore()
        for device in (*self.sides, self.partner):
            pl.semaphore_signal(barrier, inc=1, device_id=device, device_id_type=MESH)
        pl.semaphore_wait(barrier, 3)


def hops(chips, pieces):
    far = chips // 2
    orders = []
    for way in range(2):
        halves = range(pieces // 2) if way == 0 else range(pieces // 2, pieces)
        orders.append([(d, j) for d in range(1, far) for j in range(pieces)] + [(far, j) for j in halves])
    return orders


def remote(src, dst, send, recv, device):
    return pltpu.make_async_remote_copy(
        src_ref=src, dst_ref=dst, send_sem=send, recv_sem=recv, device_id=device, device_id_type=MESH
    )


def gather_kernel(grid, second, *refs):
    if second:
        x, places, taken = refs[:3]
    else:
        x, home, ids, taken, places = refs[:5]
    held_in, big, members, send, recv, give, take = refs[-7:]
    count, held = held_in.shape[:2]
    groups, group = members.shape[:2]
    width = x.shape[1]
    pieces = held // LANES
    ring = Ring(grid, count)
    orders = hops(ring.chips, pieces)
    where = [{key: t for t, key in enumerate(order)} for order in orders]
    last = len(orders[0])
    ring.greet()

    def part(block, j):
        return held_in.at[block, pl.ds(j * LANES, LANES), :]

    def widen(block, j, source):
        rows = pl.ds(pl.multiple_of(block * held + j * LANES, LANES), LANES)
        big[rows, :] = source[...].astype(jnp.float32)

    started = []

    def start(copy):
        copy.start()
        started.append(copy)

    for j in range(pieces):
        for way in range(2):
            if (1, j) in where[way]:
                t = where[way][(1, j)]
                start(
                    remote(
                        x.at[pl.ds(j * LANES, LANES), :],
                        part(ring.me, j),
                        send.at[way, t],
                        recv.at[way, t],
                        ring.sides[way],
                    )
                )
    start(remote(x, held_in.at[ring.me], give.at[0, last], take.at[0, last], ring.partner))
    for j in range(pieces):
        widen(ring.me, j, x.at[pl.ds(j * LANES, LANES), :])
    other = ring.me + 1 - 2 * ring.core

    def accept(t):
        for way in range(2):
            d, j = orders[way][t]
            block = ring.device(-d if way == 0 else d, 1 - ring.core)
            piece = part(block, j)
            remote(piece, piece, give.at[way, t], take.at[way, t], ring.partner).wait_recv()
            widen(block, j, piece)

    for t in range(last):
        for way in range(2):
            d, j = orders[way][t]
            block = ring.device(-d if way == 0 else d, ring.core)
            piece = part(block, j)
            remote(piece, piece, send.at[way, t], recv.at[way, t], ring.sides[way]).wait_recv()
            onward = where[way].get((d + 1, j))
            if onward is not None:
                start(
                    remote(
                        piece, piece, send.at[way, onward], recv.at[way, onward], ring.sides[way]
                    )
                )
            start(remote(piece, piece, give.at[way, t], take.at[way, t], ring.partner))
            widen(block, j, piece)
        if t == 2:
            remote(
                held_in.at[other], held_in.at[other], give.at[0, last], take.at[0, last], ring.partner
            ).wait_recv()
            for j in range(pieces):
                widen(other, j, part(other, j))
        if t >= LAG:
            accept(t - LAG)
    for t in range(last - LAG, last):
        accept(t)

    def gather_step(r, carry):
        base = r * group
        spots = [places[base + m] if second else home[ids[base + m]] for m in range(group)]
        if not second:
            for m in range(group):
                places[base + m] = spots[m]
        picked = [big[pl.ds(spots[m], 1), :] for m in range(group)]
        for m in range(group):
            members[r, m : m + 1, :] = picked[m]
        return carry

    lax.fori_loop(0, groups, gather_step, 0, unroll=2)

    def narrow_step(b, carry):
        some = LANES // group
        rows = pl.ds(pl.multiple_of(b * LANES, LANES), LANES)
        taken[rows, :] = members[pl.ds(b * some, some)].reshape(LANES, width).astype(taken.dtype)
        return carry

    lax.fori_loop(0, groups * group // LANES, narrow_step, 0)
    for copy in started:
        copy.wait_send()


def gather_rows(x, lists, grid, groups, group):
    count = lax.axis_size("space")
    held, width = x.shape
    entries = groups * group
    last = len(hops(count // 2, held // LANES)[0])
    sems = pltpu.SemaphoreType.DMA
    second = len(lists) == 1
    vmem = pl.BlockSpec(memory_space=pltpu.VMEM)
    smem = pl.BlockSpec(memory_space=pltpu.SMEM)
    outs = [jax.ShapeDtypeStruct((entries, width), x.dtype)]
    out_specs = [vmem]
    if not second:
        outs.append(jax.ShapeDtypeStruct((entries,), jnp.int32))
        out_specs.append(smem)
    return pl.pallas_call(
        functools.partial(gather_kernel, grid, second),
        out_shape=outs,
        in_specs=[vmem] + [smem] * len(lists),
        out_specs=out_specs,
        scratch_shapes=[
            pltpu.VMEM((count, held, width), x.dtype),
            pltpu.VMEM((count * held, width), jnp.float32),
            pltpu.VMEM((groups, group, width), jnp.float32),
            sems((2, last)),
            sems((2, last)),
            sems((2, last + 1)),
            sems((2, last + 1)),
        ],
        compiler_params=pltpu.CompilerParams(
            collective_id=2 if second else 0,
            has_side_effects=True,
            vmem_limit_bytes=60 * 1024 * 1024,
        ),
        name="spread",
    )(x, *lists)


def reduce_kernel(grid, acc, wsum, noisy, out, own, other, got, sent, wother, wgot, wsent, *sems):
    own_sem, give, take, send, recv, wgive, wtake, wsend, wrecv = sems
    chips = acc.shape[0]
    pieces = acc.shape[2] // LANES
    ring = Ring(grid, 2 * chips)
    far = chips // 2
    orders = [
        sorted(order, key=lambda key: (-key[0], key[1])) for order in hops(chips, pieces)
    ]
    where = [{key: t for t, key in enumerate(order)} for order in orders]
    last = len(orders[0])
    offsets = [far] + [s * d for d in range(far - 1, 0, -1) for s in (1, -1)] + [0]
    slot_of = {off: i for i, off in enumerate(offsets)}
    slot_of[-far] = 0
    started, local, gifts = [], [], []

    for i, off in enumerate(offsets):
        copy = pltpu.make_async_copy(acc.at[ring.chip(off), ring.core], own.at[i], own_sem.at[i])
        copy.start()
        local.append(copy)
    ring.greet()
    for i, off in enumerate(offsets):
        copy = remote(
            acc.at[ring.chip(off), 1 - ring.core], other.at[i], give.at[i], take.at[i], ring.partner
        )
        copy.start()
        gifts.append(copy)
        if i == 0:
            wgift = remote(wsum, wother, wgive.at[0], wtake.at[0], ring.partner)
            wgift.start()
    ready = set()

    def settle_slot(i):
        if i not in ready:
            ready.add(i)
            local[i].wait()
            gifts[i].wait_recv()

    def value(off, j, ways, d):
        i = slot_of[off]
        settle_slot(i)
        rows = pl.ds(j * LANES, LANES)
        total = own[i, rows, :].astype(jnp.float32) + other[i, rows, :].astype(jnp.float32)
        for way in ways:
            t = where[way].get((d + 1, j))
            if t is not None:
                piece = got.at[way, t]
                remote(sent.at[way, t], piece, send.at[way, t], recv.at[way, t], ring.sides[way]).wait_recv()
                total = total + piece[...].astype(jnp.float32)
        return total

    def weights(off, ways, d):
        chip = ring.chip(off)
        if "w" not in ready:
            ready.add("w")
            wgift.wait_recv()
        total = wsum[chip, ring.core] + wother[chip, ring.core]
        for way in ways:
            if d + 1 < far or (d + 1 == far and way == 0):
                remote(
                    wsent.at[way, d + 1],
                    wgot.at[way, d + 1],
                    wsend.at[way, d + 1],
                    wrecv.at[way, d + 1],
                    ring.sides[way],
                ).wait_recv()
                total = total + wgot[way, d + 1]
        return total

    for t in range(last):
        for way in range(2):
            d, j = orders[way][t]
            off = d if way == 0 else -d
            sent[way, t] = value(off, j, (way,), d).astype(sent.dtype)
            copy = remote(sent.at[way, t], got.at[way, t], send.at[way, t], recv.at[way, t], ring.sides[way])
            copy.start()
            started.append(copy)
            final_piece = t + 1 == last or orders[way][t + 1][0] != d
            if final_piece and (d < far or way == 0):
                wsent[way, d] = weights(off, (way,), d)
                copy = remote(
                    wsent.at[way, d], wgot.at[way, d], wsend.at[way, d], wrecv.at[way, d], ring.sides[way]
                )
                copy.start()
                started.append(copy)
    lane = lax.broadcasted_iota(jnp.int32, (LANES, LANES), 1)
    sub = lax.broadcasted_iota(jnp.int32, (LANES, LANES), 0)
    denom = weights(0, (0, 1), 0)
    for j in range(pieces):
        rows = pl.ds(j * LANES, LANES)
        numer = value(0, j, (0, 1), 0) + prior_weight * noisy[rows, :].astype(jnp.float32)
        spread = jnp.broadcast_to(denom[j : j + 1, :], (LANES, LANES))
        column = jnp.sum(jnp.where(lane == sub, spread, 0.0), axis=1, keepdims=True)
        out[rows, :] = (numer / (column + prior_weight)).astype(out.dtype)
    for copy in started + gifts + [wgift]:
        copy.wait_send()


def settle(acc, wsum, noisy, grid):
    count = lax.axis_size("space")
    held, width = noisy.shape
    chips, pieces = count // 2, held // LANES
    far = chips // 2
    last = len(hops(chips, pieces)[0])
    sems = pltpu.SemaphoreType.DMA
    vmem = pl.BlockSpec(memory_space=pltpu.VMEM)
    small = (chips, 2, pieces, LANES)
    return pl.pallas_call(
        functools.partial(reduce_kernel, grid),
        out_shape=jax.ShapeDtypeStruct(noisy.shape, noisy.dtype),
        in_specs=[pl.BlockSpec(memory_space=pltpu.HBM), vmem, vmem],
        out_specs=vmem,
        scratch_shapes=[
            pltpu.VMEM((chips, held, width), acc.dtype),
            pltpu.VMEM((chips, held, width), acc.dtype),
            pltpu.VMEM((2, last, LANES, width), acc.dtype),
            pltpu.VMEM((2, last, LANES, width), acc.dtype),
            pltpu.VMEM(small, jnp.float32),
            pltpu.VMEM((2, far + 1, pieces, LANES), jnp.float32),
            pltpu.VMEM((2, far + 1, pieces, LANES), jnp.float32),
            sems((chips,)),
            sems((chips,)),
            sems((chips,)),
            sems((2, last)),
            sems((2, last)),
            sems((1,)),
            sems((1,)),
            sems((2, far + 1)),
            sems((2, far + 1)),
        ],
        compiler_params=pltpu.CompilerParams(
            collective_id=1, has_side_effects=True, vmem_limit_bytes=60 * 1024 * 1024
        ),
        name="settle",
    )(acc.reshape(chips, 2, held, width), wsum.reshape(small), noisy)


def body(grid, noisy, matches, cube_home, sigma_coef):
    groups, group = matches.shape
    cubes = cube_home.shape[0]
    tables = make_tables(group)
    sigma = sigma_coef[None, :]
    members, rows = gather_rows(noisy, (cube_home, matches.reshape(-1)), grid, groups, group)
    coeffs, acc, wsum = phase(False, rows, sigma, tables, members, cubes, group)
    basic = settle(acc, wsum, noisy, grid)
    (guide,) = gather_rows(basic, (rows,), grid, groups, group)
    acc2, wsum2 = phase(True, rows, sigma, tables, guide, cubes, group, coeffs)
    return basic, settle(acc2, wsum2, noisy, grid)


def solution(mesh):
    in_specs = (P(("groups", "space"), None), P(("groups", "space"), None), P("groups"), P())
    out_specs = (P(("groups", "space"), None), P(("groups", "space"), None))
    grid = 2 if mesh.shape["groups"] == 2 else 1
    return jax.shard_map(
        functools.partial(body, grid),
        mesh=mesh,
        in_specs=in_specs,
        out_specs=out_specs,
        check_vma=False,
    )
```

profile of v0, /device:TPU:0, one launch (start us, length us, event | category | flops | bytes accessed | tf_op | source)
XLA Modules:
  0.0 250.5 jit_solution(8433422179197715173)
XLA Ops:
  0.6 0.8 copy.10
  1.4 0.7 reshape.19.refs_2_
  2.1 52.9 %spread.2 = (bf16[1536,512]{1,0:T(8,128)(2,1)}, s32[1536]{0:T(1024)}) custom-call(bf16[512,512]{1,0:T(8,128)(2,1)} %noisy.3, s32[8192]{0:T(1024)} %refs_1_.1, s32[1536]{0:T(1024)} %reshape.19.refs_2_), custom_call_target="tpu_custom_call" | custom-call | tf_op jit(solution)/shard_map/spread/pallas_call | solution.py:358
  55.0 23.2 %shrink.1 = (f32[1536,512]{1,0:T(8,128)}, bf16[8192,512]{1,0:T(8,128)(2,1)}, f32[64,128]{1,0:T(8,128)}) custom-call(s32[1536]{0:T(1024)} %get-tuple-element.9.refs_0_.refs_1_, f32[1,512]{1,0:T(1,128)} %bitcast.9, bf16[512,512]{1,0:T(8,128)(2,1)} %constant.8.clone.refs_2_, bf16[512,512]{1,0:T(8,128)(2,1)} %constant.9.clone.refs_3_, ...), custom_call_target="tpu_custom_call" | custom-call | tf_op jit(solution)/shard_map/shrink/pallas_call | solution.py:173
  78.2 49.1 %settle.2.refs_0_ = bf16[512,512]{1,0:T(8,128)(2,1)} custom-call(bf16[8,2,512,512]{3,2,1,0:T(8,128)(2,1)} %bitcast.6, f32[8,2,4,128]{3,2,1,0:T(4,128)} %bitcast.8, bf16[512,512]{1,0:T(8,128)(2,1)} %noisy.3), custom_call_target="tpu_custom_call" | custom-call | tf_op jit(solution)/shard_map/settle/pallas_call | solution.py:488
  127.3 49.0 %spread.3.refs_6_ = bf16[1536,512]{1,0:T(8,128)(2,1)} custom-call(bf16[512,512]{1,0:T(8,128)(2,1)} %settle.2.refs_0_, s32[1536]{0:T(1024)} %get-tuple-element.9.refs_0_.refs_1_), custom_call_target="tpu_custom_call" | custom-call | tf_op jit(solution)/shard_map/spread/pallas_call | solution.py:358
  176.3 23.2 %wiener.1 = (bf16[8192,512]{1,0:T(8,128)(2,1)}, f32[64,128]{1,0:T(8,128)}) custom-call(s32[1536]{0:T(1024)} %get-tuple-element.9.refs_0_.refs_1_, f32[1,512]{1,0:T(1,128)} %bitcast.10, bf16[512,512]{1,0:T(8,128)(2,1)} %constant.8.clone.refs_2_, bf16[512,512]{1,0:T(8,128)(2,1)} %constant.9.clone.refs_3_, bf16[128,256]{1,0:T(8,128)(2,1)} %constant.10.clone.refs_4_, ...), custom_call_target="tpu_custom_call" | custom-call | tf_op jit(solution)/shard_map/wiener/pallas_call | solution.py:173
  199.5 0.0 copy-start
  199.5 48.4 %settle.3 = bf16[512,512]{1,0:T(8,128)(2,1)} custom-call(bf16[8,2,512,512]{3,2,1,0:T(8,128)(2,1)} %bitcast.5, f32[8,2,4,128]{3,2,1,0:T(4,128)} %bitcast.7, bf16[512,512]{1,0:T(8,128)(2,1)} %noisy.3), custom_call_target="tpu_custom_call" | custom-call | tf_op jit(solution)/shard_map/settle/pallas_call | solution.py:488
  247.9 0.0 copy-done
  247.9 0.8 copy.13
  248.7 1.9 copy.14
Async XLA Ops:
  199.5 48.4 %copy-start = (bf16[512,512]{1,0:T(8,128)(2,1)S(1)}, bf16[512,512]{1,0:T(8,128)(2,1)}, u32[]{:S(2)}) copy-start(bf16[512,512]{1,0:T(8,128)(2,1)} %settle.2.refs_0_) | copy-start | bytes 1572868
where the time goes:
time: 251 us
  Pallas kernels  246 us (98%)
  local copies, waits for them, and re-layouts  4.14 us (2%)
    pallas_call x2, Pallas kernels, gather_rows(): pl.pallas_call(functools.partial(gather_kernel, grid, second), out_shape=...  102 us
    pallas_call x2, Pallas kernels, settle(): pl.pallas_call(functools.partial(reduce_kernel, grid), out_shape=jax.Shap...  97.4 us
    pallas_call x2, Pallas kernels, phase(): pl.pallas_call(functools.partial(kernel, second, group), out_shape=outs,...  46.4 us

commit v1 on v0

v1 whole, which is shorter than its diff:
```python
import functools

import jax
import jax.numpy as jnp
import numpy as np
from jax import lax
from jax.experimental import pallas as pl
from jax.experimental.pallas import tpu as pltpu
from jax.sharding import PartitionSpec as P

shrink_level = 2.7
prior_weight = 0.5
LANES = 128
SUBS = 8
PIECES = 2
STREAMS = 4
TOGETHER = 2
LIMIT = 60 * 1024 * 1024
MESH = pl.DeviceIdType.MESH
VMEM = pl.BlockSpec(memory_space=pltpu.VMEM)
SMEM = pl.BlockSpec(memory_space=pltpu.SMEM)
HBM = pl.BlockSpec(memory_space=pltpu.HBM)
SEMS = pltpu.SemaphoreType.DMA


def dct_matrix(length):
    index = np.arange(length, dtype=np.float64)
    table = np.cos(np.pi * (2.0 * index[None, :] + 1.0) * index[:, None] / (2.0 * length))
    table = table * np.sqrt(2.0 / length)
    table[0] /= np.sqrt(2.0)
    return table


def cube_tables():
    small = dct_matrix(8)
    cube = np.kron(np.kron(small, small), small).astype(np.float32)
    return cube.astype(jnp.bfloat16), cube.T.astype(jnp.bfloat16)


def half_cosines(n):
    return [float(2.0 * np.cos(np.pi * (2 * i + 1) / (2 * n))) for i in range(n // 2)]


def cosine_sums(x):
    n = len(x)
    if n == 2:
        return [x[0] + x[1], (x[0] - x[1]) * float(np.cos(np.pi / 4))]
    half = n // 2
    even = cosine_sums([x[i] + x[n - 1 - i] for i in range(half)])
    turned = cosine_sums([(x[i] - x[n - 1 - i]) * f for i, f in enumerate(half_cosines(n))])
    out = [None] * n
    for k in range(half):
        out[2 * k] = even[k]
        out[2 * k + 1] = turned[k] - out[2 * k - 1] if k else 0.5 * turned[0]
    return out


def cosine_sums_transposed(y):
    n = len(y)
    if n == 2:
        odd = y[1] * float(np.cos(np.pi / 4))
        return [y[0] + odd, y[0] - odd]
    half = n // 2
    even = cosine_sums_transposed(y[0::2])
    tail = [None] * half
    for k in reversed(range(half)):
        tail[k] = y[2 * k + 1] - tail[k + 1] if k + 1 < half else y[2 * k + 1]
    tail[0] = 0.5 * tail[0]
    odd = [o * f for o, f in zip(cosine_sums_transposed(tail), half_cosines(n))]
    return [even[i] + odd[i] for i in range(half)] + [even[i] - odd[i] for i in reversed(range(half))]


def scales(n):
    return [float(np.sqrt((1.0 if k == 0 else 2.0) / n)) for k in range(n)]


def flip(value, mask):
    bit = 1
    while bit <= mask:
        if mask & bit:
            value = value + bit - 2 * bit * lax.rem(value // bit, 2)
        bit *= 2
    return value


def lowest(d, count):
    return d & -d if d else count


class Place:
    def __init__(self, count, parts):
        self.parts, self.ranks = parts, count // parts
        me = lax.axis_index("space")
        self.part, self.rank = me // self.ranks, lax.rem(me, self.ranks)
        self.bits = [1 << b for b in range(self.ranks.bit_length() - 1)]

    def index(self, off, d):
        return flip(self.part, off) * self.ranks + flip(self.rank, d)

    def device(self, off, d):
        return {"space": self.index(off, d)}

    def greet(self):
        barrier = pltpu.get_barrier_semaphore()
        peers = [(off, 0) for off in range(1, self.parts)] + [(0, d) for d in range(1, self.ranks)]
        for off, d in peers:
            pl.semaphore_signal(barrier, inc=1, device_id=self.device(off, d), device_id_type=MESH)
        pl.semaphore_wait(barrier, len(peers))


def remote(src, dst, send, recv, device):
    return pltpu.make_async_remote_copy(
        src_ref=src, dst_ref=dst, send_sem=send, recv_sem=recv, device_id=device, device_id_type=MESH
    )


def piece_of(ref, h):
    size = ref.shape[0] // PIECES
    return ref.at[pl.ds(h * size, size), :]


class Spread:
    def __init__(self, place, stage, got, table, send, recv):
        self.place, self.stage, self.got, self.table = place, stage, got, table
        self.send, self.recv, self.started = send, recv, []

    def block(self, off, d):
        return self.stage.at[0] if off == 0 and d == 0 else self.got.at[off, d]

    def pass_on(self, off, d, h):
        place = self.place
        for bit in reversed(place.bits):
            if bit < lowest(d, place.ranks):
                copy = remote(
                    piece_of(self.block(off, d), h),
                    piece_of(self.got.at[off, d | bit], h),
                    self.send.at[off, d | bit, h],
                    self.recv.at[off, d | bit, h],
                    place.device(0, bit),
                )
                copy.start()
                self.started.append(copy)

    def begin(self, rows, cube_t):
        place = self.place
        for off in list(range(place.parts - 1, 0, -1)) + [0]:
            columns = pl.ds(pl.multiple_of(flip(place.part, off) * LANES, LANES), LANES)
            spec = jnp.dot(rows, cube_t[:, columns], preferred_element_type=jnp.float32)
            self.stage[off] = spec.astype(self.stage.dtype)
            for h in range(PIECES):
                if off == 0:
                    self.pass_on(0, 0, h)
                    continue
                copy = remote(
                    piece_of(self.stage.at[off], h),
                    piece_of(self.got.at[off, 0], h),
                    self.send.at[off, 0, h],
                    self.recv.at[off, 0, h],
                    place.device(off, 0),
                )
                copy.start()
                self.started.append(copy)

    def widen(self, off, d, h):
        source = piece_of(self.block(off, d), h)
        held = self.stage.shape[1]
        size = held // PIECES
        first = self.place.index(off, d) * held + h * size
        rows = pl.ds(pl.multiple_of(first, size), size)
        self.table[rows, :] = source[...].astype(jnp.float32)

    def finish(self):
        place = self.place

        def when(key):
            off, d, h = key
            return (place.parts - off if off else 0) + 0.5 * h + sum(0.3 if b == 1 else 1.0 for b in place.bits if d & b)

        keys = [
            (off, d, h)
            for off in range(place.parts)
            for d in range(place.ranks)
            for h in range(PIECES)
            if off or d
        ]
        for h in range(PIECES):
            self.widen(0, 0, h)
        for off, d, h in sorted(keys, key=when):
            piece = piece_of(self.got.at[off, d], h)
            remote(
                piece, piece, self.send.at[off, d, h], self.recv.at[off, d, h], place.device(off, d)
            ).wait_recv()
            self.pass_on(off, d, h)
            self.widen(off, d, h)

    def close(self):
        for copy in self.started:
            copy.wait_send()


def spread_scratch(count, parts, held, dtype):
    ranks = count // parts
    return [
        pltpu.VMEM((parts, held, LANES), dtype),
        pltpu.VMEM((parts, ranks, held, LANES), dtype),
        pltpu.VMEM((count * held, LANES), jnp.float32),
        SEMS((parts, ranks, PIECES)),
        SEMS((parts, ranks, PIECES)),
    ]


def pick_rows(table, lists, members, some):
    parts, group = lists.shape[:2]
    for src in range(parts):

        def step(q, carry):
            for m in range(group):
                members[m, pl.ds(src * some + q, 1), :] = table[pl.ds(lists[src, m, q], 1), :]
            return carry

        lax.fori_loop(0, some, step, 0, unroll=4)


def diagonal(rows):
    shape = (rows, LANES)
    return lax.broadcasted_iota(jnp.int32, shape, 0) == lax.broadcasted_iota(jnp.int32, shape, 1)


def shrink_groups(place, second, width, some, sigma, members, coeffs, back, energy, ebuf, egot, weights, send, recv):
    group, refs = members.shape[:2]
    factor = scales(group)
    columns = pl.ds(pl.multiple_of(place.part * LANES, LANES), LANES)
    own = sigma[:, columns]
    level = own * own if second else (shrink_level * own) * (shrink_level * own)

    def forward(b, carry):
        rows = pl.ds(pl.multiple_of(b * SUBS, SUBS), SUBS)
        values = cosine_sums([members[m, rows, :] for m in range(group)])
        total = None
        for j in range(group):
            value = values[j] * factor[j]
            square = value * value
            gain = square / (square + level)
            power = gain * gain
            total = power if total is None else total + power
            if second:
                members[j, rows, :] = gain * coeffs[j, rows, :]
            else:
                coeffs[j, rows, :] = value
                members[j, rows, :] = gain * value
        energy[rows, :] = total * level if second else total
        return carry

    lax.fori_loop(0, refs // SUBS, forward, 0)
    parts = refs // some
    for src in range(parts):
        column = jnp.sum(energy[src * some : (src + 1) * some, :], axis=1, keepdims=True)
        ebuf[src : src + 1, :] = jnp.sum(jnp.where(diagonal(some), column, 0.0), axis=0, keepdims=True)
    started = []
    for off in range(1, place.parts):
        copy = remote(ebuf, egot.at[off], send.at[off], recv.at[off], place.device(off, 0))
        copy.start()
        started.append(copy)

    def inverse(b, carry):
        rows = pl.ds(pl.multiple_of(b * 2 * SUBS, 2 * SUBS), 2 * SUBS)
        values = cosine_sums_transposed([members[j, rows, :] * factor[j] for j in range(group)])
        for m in range(group):
            back[m, rows, :] = values[m].astype(back.dtype)
        return carry

    lax.fori_loop(0, refs // (2 * SUBS), inverse, 0)
    total = ebuf[...]
    for off in range(1, place.parts):
        remote(ebuf, egot.at[off], send.at[off], recv.at[off], place.device(off, 0)).wait_recv()
        total = total + egot[off]
    weights[...] = 1.0 / (0.25 + total / (group * width))
    for copy in started:
        copy.wait_send()


def shrink_scratch(parts, group, refs):
    assert parts <= SUBS
    return [
        pltpu.VMEM((group, refs, LANES), jnp.float32),
        pltpu.VMEM((refs, LANES), jnp.float32),
        pltpu.VMEM((SUBS, LANES), jnp.float32),
        pltpu.VMEM((parts, SUBS, LANES), jnp.float32),
        SEMS((parts,)),
        SEMS((parts,)),
    ]


def first_kernel(count, x, home, ids, sigma, cube_t, coeffs, back, weights, lists_out, *scratch):
    stage, got, table, send, recv = scratch[:5]
    members, energy, ebuf, egot, esend, erecv = scratch[5:11]
    named, lists_v, lists_s, lsend, lrecv, lsem = scratch[11:]
    parts = stage.shape[0]
    group, some = ids.shape
    place = Place(count, parts)
    place.greet()
    spread = Spread(place, stage, got, table, send, recv)
    spread.begin(x[...], cube_t)

    def look_up(m, carry):
        for q in range(some):
            named[m, q] = home[ids[m, q]]
        for q in range(some, LANES):
            named[m, q] = 0
        return carry

    lax.fori_loop(0, group, look_up, 0)
    ebuf[...] = jnp.zeros(ebuf.shape, ebuf.dtype)
    mine = pltpu.make_async_copy(named, lists_v.at[place.part], lsem.at[0])
    mine.start()
    mine.wait()
    started = []
    for off in range(1, parts):
        copy = remote(
            lists_v.at[place.part],
            lists_v.at[place.part],
            lsend.at[off],
            lrecv.at[off],
            place.device(off, 0),
        )
        copy.start()
        started.append(copy)
    spread.finish()
    copies = []
    for off in range(parts):
        source = lists_v.at[flip(place.part, off)]
        if off:
            remote(source, source, lsend.at[off], lrecv.at[off], place.device(off, 0)).wait_recv()
        copy = pltpu.make_async_copy(source, lists_s.at[flip(place.part, off)], lsem.at[off])
        copy.start()
        copies.append(copy)
    for copy in copies:
        copy.wait()
    lists_out[...] = lists_v[...]
    pick_rows(table, lists_s, members, some)
    shrink_groups(
        place, False, x.shape[1], some, sigma, members, coeffs, back, energy, ebuf, egot, weights, esend, erecv
    )
    for copy in started:
        copy.wait_send()
    spread.close()


class Collect:
    def __init__(self, place, acc, own, got, sent, zgot, local, send, recv):
        self.place, self.acc, self.own, self.got, self.sent, self.zgot = place, acc, own, got, sent, zgot
        self.local, self.send, self.recv, self.started = local, send, recv, []
        self.order = list(range(place.parts - 1, -1, -1))

    def start(self, copy):
        copy.start()
        self.started.append(copy)

    def fetch(self, off, d):
        return pltpu.make_async_copy(
            self.acc.at[self.place.index(off, d)], self.own.at[off, d // 2], self.local.at[off, d // 2]
        )

    def open(self):
        place = self.place
        for d in sorted(range(0, place.ranks, 2), key=lambda d: lowest(d, place.ranks)):
            for off in self.order:
                self.fetch(off, d).start()

    def begin(self):
        place = self.place
        for d in sorted(range(1, place.ranks, 2), key=lambda d: lowest(d - 1, place.ranks)):
            for off in self.order:
                for h in range(PIECES):
                    self.start(
                        remote(
                            piece_of(self.acc.at[place.index(off, d)], h),
                            piece_of(self.got.at[off, d], h),
                            self.send.at[off, d, h],
                            self.recv.at[off, d, h],
                            place.device(0, 1),
                        )
                    )

    def value(self, off, d, h):
        place = self.place
        if h == 0:
            self.fetch(off, d).wait()
        total = piece_of(self.own.at[off, d // 2], h)[...].astype(jnp.float32)
        for bit in place.bits:
            if bit < lowest(d, place.ranks):
                piece = piece_of(self.got.at[off, d | bit], h)
                remote(
                    piece, piece, self.send.at[off, d | bit, h], self.recv.at[off, d | bit, h], place.device(0, bit)
                ).wait_recv()
                total = total + piece[...].astype(jnp.float32)
        return total

    def run(self):
        place = self.place
        for d in sorted(range(0, place.ranks, 2), key=lambda d: lowest(d, place.ranks)):
            for off in self.order:
                for h in range(PIECES):
                    piece = piece_of(self.sent.at[off, d // 2], h)
                    piece[...] = self.value(off, d, h).astype(self.sent.dtype)
                    if d == 0 and off == 0:
                        continue
                    bit = lowest(d, 0)
                    self.start(
                        remote(
                            piece,
                            piece_of(self.got.at[off, d] if d else self.zgot.at[off], h),
                            self.send.at[off, d, h],
                            self.recv.at[off, d, h],
                            place.device(0, bit) if d else place.device(off, 0),
                        )
                    )

    def slices(self, h):
        place = self.place
        yield 0, piece_of(self.sent.at[0, 0], h)[...]
        for off in self.order[:-1]:
            piece = piece_of(self.zgot.at[off], h)
            remote(
                piece, piece, self.send.at[off, 0, h], self.recv.at[off, 0, h], place.device(off, 0)
            ).wait_recv()
            yield off, piece[...]

    def close(self):
        for copy in self.started:
            copy.wait_send()


def settle(place, acc, wsum, noisy, cube, out, own, got, sent, zgot, wgot, local, send, recv, wsend, wrecv):
    held = noisy.shape[0]
    collect = Collect(place, acc, own, got, sent, zgot, local, send, recv)
    collect.open()
    place.greet()
    collect.begin()
    for d in range(1, place.ranks):
        collect.start(
            remote(wsum.at[flip(place.rank, d)], wgot.at[d], wsend.at[d], wrecv.at[d], place.device(0, d))
        )
    collect.run()
    denom = wsum[place.rank]
    for d in range(1, place.ranks):
        remote(wgot.at[d], wgot.at[d], wsend.at[d], wrecv.at[d], place.device(0, d)).wait_recv()
        denom = denom + wgot[d]
    size = held // PIECES
    for h in range(PIECES):
        numer = prior_weight * noisy[pl.ds(h * size, size), :].astype(jnp.float32)
        for off, part in collect.slices(h):
            rows = pl.ds(pl.multiple_of(flip(place.part, off) * LANES, LANES), LANES)
            numer = numer + jnp.dot(part, cube[rows, :], preferred_element_type=jnp.float32)
        for j in range(size // LANES):
            row = h * (size // LANES) + j
            spread = jnp.broadcast_to(denom[row : row + 1, :], (LANES, LANES))
            column = jnp.sum(jnp.where(diagonal(LANES), spread, 0.0), axis=1, keepdims=True)
            out[pl.ds(row * LANES, LANES), :] = (
                numer[j * LANES : (j + 1) * LANES, :] / (column + prior_weight)
            ).astype(out.dtype)
    return collect


def settle_scratch(count, parts, held, dtype):
    ranks = count // parts
    half = (parts, ranks // 2, held, LANES)
    return [
        pltpu.VMEM(half, dtype),
        pltpu.VMEM((parts, ranks, held, LANES), dtype),
        pltpu.VMEM(half, dtype),
        pltpu.VMEM((parts, held, LANES), dtype),
        pltpu.VMEM((ranks, SUBS, LANES), jnp.float32),
        SEMS((parts, ranks // 2)),
        SEMS((parts, ranks, PIECES)),
        SEMS((parts, ranks, PIECES)),
        SEMS((ranks,)),
        SEMS((ranks,)),
    ]


def second_kernel(count, some, acc, wsum, noisy, cube, cube_t, sigma, lists, coeffs_in, basic, back, weights, *scratch):
    stage, got, table, send, recv = scratch[:5]
    members, energy, ebuf, egot, esend, erecv = scratch[5:11]
    coeffs, csem = scratch[11:13]
    parts = stage.shape[0]
    place = Place(count, parts)
    fetch = pltpu.make_async_copy(coeffs_in, coeffs, csem.at[0])
    fetch.start()
    collect = settle(place, acc, wsum, noisy, cube, basic, *scratch[13:])
    spread = Spread(place, stage, got, table, send, recv)
    spread.begin(basic[...], cube_t)
    ebuf[...] = jnp.zeros(ebuf.shape, ebuf.dtype)
    spread.finish()
    pick_rows(table, lists, members, some)
    fetch.wait()
    shrink_groups(
        place, True, noisy.shape[1], some, sigma, members, coeffs, back, energy, ebuf, egot, weights, esend, erecv
    )
    collect.close()
    spread.close()


def third_kernel(count, parts, acc, wsum, noisy, cube, out, *scratch):
    settle(Place(count, parts), acc, wsum, noisy, cube, out, *scratch).close()


def add_kernel(count, some, lists, lists_v, weights, back, acc, wsum, members, *sums):
    parts, group = lists.shape[:2]
    place = Place(count, parts)
    blocks, held = acc.shape[:2]

    def clear(i, carry):
        rows = pl.ds(pl.multiple_of(i * LANES, LANES), LANES)
        for each in sums:
            each[rows, :] = jnp.zeros((LANES, LANES), jnp.float32)
        return carry

    lax.fori_loop(0, blocks * held // LANES, clear, 0)
    for src in range(parts):
        row = jnp.broadcast_to(weights[src : src + 1, :], (some, LANES))
        column = jnp.sum(jnp.where(diagonal(some), row, 0.0), axis=1, keepdims=True)
        spread = jnp.broadcast_to(column, (some, LANES))
        rows = pl.ds(src * some, some)

        def scale(m, carry):
            members[m, rows, :] = back[m, rows, :].astype(jnp.float32) * spread
            return carry

        lax.fori_loop(0, group, scale, 0)

    many = wsum.shape[0] * (held // LANES)
    lane = lax.broadcasted_iota(jnp.int32, (1, LANES), 1)
    heavy = [jnp.where(lane < some, weights[src : src + 1, :], 0.0) for src in range(parts)]
    tall = lax.broadcasted_iota(jnp.int32, (many, LANES), 0)
    low = lax.broadcasted_iota(jnp.int32, (LANES, LANES), 0)
    first = place.part * (many * LANES)

    def weigh(m, total):
        ones, loads = [], []
        for src in range(parts):
            spots = lists_v[src, pl.ds(m, 1), :] - first
            loads.append(jnp.where((spots >> 7) == tall, heavy[src], 0.0).astype(jnp.bfloat16))
            ones.append(jnp.where((spots & (LANES - 1)) == low, 1.0, 0.0).astype(jnp.bfloat16))
        return total + lax.dot_general(
            jnp.concatenate(loads, axis=1),
            jnp.concatenate(ones, axis=1),
            (((1,), (1,)), ((), ())),
            preferred_element_type=jnp.float32,
        )

    total = lax.fori_loop(0, group, weigh, jnp.zeros((many, LANES), jnp.float32))
    per = held // LANES
    for b in range(wsum.shape[0]):
        wsum[b, :per, :] = total[b * per : (b + 1) * per, :]
        if per < SUBS:
            wsum[b, per:, :] = jnp.zeros((SUBS - per, LANES), jnp.float32)

    for src in range(parts):

        def step(q, carry):
            for base in range(0, group, STREAMS * TOGETHER):
                spots, news = [], []
                for s in range(STREAMS):
                    ms = [base + s * TOGETHER + t for t in range(TOGETHER)]
                    where = [lists[src, m, q] for m in ms]
                    extra = [members[m, pl.ds(src * some + q, 1), :] for m in ms]
                    fresh = [sums[s][pl.ds(w, 1), :] + e for w, e in zip(where, extra)]
                    for t in range(TOGETHER):
                        for u in range(t):
                            fresh[t] = fresh[t] + jnp.where(where[u] == where[t], extra[u], 0.0)
                    spots.append(where)
                    news.append(fresh)
                for s in range(STREAMS):
                    for w, n in zip(spots[s], news[s]):
                        sums[s][pl.ds(w, 1), :] = n
            return carry

        lax.fori_loop(0, some, step, 0, unroll=2)

    def store(b, carry):
        for i in range(held // LANES):
            rows = pl.ds(pl.multiple_of(b * held + i * LANES, LANES), LANES)
            whole = sums[0][rows, :]
            for each in sums[1:]:
                whole = whole + each[rows, :]
            acc[b, i * LANES : (i + 1) * LANES, :] = whole.astype(acc.dtype)
        return carry

    lax.fori_loop(0, blocks, store, 0)


def shape(*dims, dtype=jnp.float32):
    return jax.ShapeDtypeStruct(dims, dtype)


def params(collective_id=None):
    return pltpu.CompilerParams(
        collective_id=collective_id, has_side_effects=collective_id is not None, vmem_limit_bytes=LIMIT
    )


def add_up(count, some, held, lists, weights, back):
    parts, group = lists.shape[:2]
    ranks = count // parts
    return pl.pallas_call(
        functools.partial(add_kernel, count, some),
        out_shape=[shape(count, held, LANES, dtype=back.dtype), shape(ranks, SUBS, LANES)],
        in_specs=[SMEM, VMEM, VMEM, VMEM],
        out_specs=[VMEM, VMEM],
        scratch_shapes=[pltpu.VMEM((group, parts * some, LANES), jnp.float32)]
        + [pltpu.VMEM((count * held, LANES), jnp.float32)] * STREAMS,
        compiler_params=params(),
        name="add_up",
    )(lists, lists, weights, back)


def body(noisy, matches, cube_home, sigma_coef):
    count = lax.axis_size("space")
    some, group = matches.shape
    held, width = noisy.shape
    parts = width // LANES
    refs = parts * some
    cube, cube_t = cube_tables()
    sigma = sigma_coef[None, :]
    dtype = noisy.dtype
    shared = spread_scratch(count, parts, held, dtype) + shrink_scratch(parts, group, refs)
    coeffs, back, weights, lists = pl.pallas_call(
        functools.partial(first_kernel, count),
        out_shape=[
            shape(group, refs, LANES),
            shape(group, refs, LANES, dtype=dtype),
            shape(SUBS, LANES),
            shape(parts, group, LANES, dtype=jnp.int32),
        ],
        in_specs=[VMEM, SMEM, SMEM, VMEM, VMEM],
        out_specs=[VMEM] * 4,
        scratch_shapes=shared
        + [
            pltpu.SMEM((group, LANES), jnp.int32),
            pltpu.VMEM((parts, group, LANES), jnp.int32),
            pltpu.SMEM((parts, group, LANES), jnp.int32),
            SEMS((parts,)),
            SEMS((parts,)),
            SEMS((parts,)),
        ],
        compiler_params=params(0),
        name="shrink",
    )(noisy, cube_home, matches.T, sigma, cube_t)
    acc, wsum = add_up(count, some, held, lists, weights, back)
    basic, back, weights = pl.pallas_call(
        functools.partial(second_kernel, count, some),
        out_shape=[
            shape(held, width, dtype=dtype),
            shape(group, refs, LANES, dtype=dtype),
            shape(SUBS, LANES),
        ],
        in_specs=[HBM] + [VMEM] * 5 + [SMEM, HBM],
        out_specs=[VMEM] * 3,
        scratch_shapes=shared
        + [pltpu.VMEM((group, refs, LANES), jnp.float32), SEMS((1,))]
        + settle_scratch(count, parts, held, dtype),
        compiler_params=params(1),
        name="wiener",
    )(acc, wsum, noisy, cube, cube_t, sigma, lists, coeffs)
    acc, wsum = add_up(count, some, held, lists, weights, back)
    final = pl.pallas_call(
        functools.partial(third_kernel, count, parts),
        out_shape=shape(held, width, dtype=dtype),
        in_specs=[HBM] + [VMEM] * 3,
        out_specs=VMEM,
        scratch_shapes=settle_scratch(count, parts, held, dtype),
        compiler_params=params(2),
        name="settle",
    )(acc, wsum, noisy, cube)
    return basic, final


def solution(mesh):
    in_specs = (P(("groups", "space"), None), P(("groups", "space"), None), P("groups"), P())
    out_specs = (P(("groups", "space"), None), P(("groups", "space"), None))
    return jax.shard_map(body, mesh=mesh, in_specs=in_specs, out_specs=out_specs, check_vma=False)
```

time: 251 us -> 169 us (0.67)
  Pallas kernels: 246 us -> 165 us
    pallas_call x6 -> x5, Pallas kernels: 246 us -> 165 us  [the longest x1 56.5 us: body(): pl.pallas_call(functools.partial(second_kernel, count, some), out_shape=[...]
where the time goes in v1:
time: 169 us; the launch traced here: 168 us
  Pallas kernels  165 us (98%)
  local copies, waits for them, and re-layouts  2.67 us (2%)
    pallas_call x1, Pallas kernels, body(): pl.pallas_call(functools.partial(second_kernel, count, some), out_shape=[...  56.5 us
    pallas_call x1, Pallas kernels, body(): pl.pallas_call(functools.partial(first_kernel, count), out_shape=[shape(g...  46.8 us
    pallas_call x2, Pallas kernels, add_up(): pl.pallas_call(functools.partial(add_kernel, count, some), out_shape=[sha...  39.5 us
    pallas_call x1, Pallas kernels, body(): pl.pallas_call(functools.partial(third_kernel, count, parts), out_shape=s...  22.2 us

profile of v1, /device:TPU:0, one launch (start us, length us, event | category | flops | bytes accessed | tf_op | source)
XLA Modules:
  0.0 168.3 jit_solution(3429584866791140784)
XLA Ops:
  0.6 46.8 %shrink.1 = (f32[16,384,128]{2,1,0:T(8,128)}, bf16[16,384,128]{2,1,0:T(8,128)(2,1)}, f32[8,128]{1,0:T(8,128)}, s32[4,16,128]{2,1,0:T(8,128)}) custom-call(bf16[512,512]{1,0:T(8,128)(2,1)} %noisy.3, s32[8192]{0:T(1024)} %home.1, s32[16,96]{1,0:T(8,128)} %bitcast.4, f32[1,512]{1,0:T(1,128)} %bitcast.2, bf16[512,512]{1,0:T(8,128)(2,1)} %constant.4.clone.cube_t), custom_call_target="tpu_custom_call" | custom-call | tf_op jit(solution)/shard_map/shrink/pallas_call | solution.py:628
  47.4 19.8 %add_up.2 = (bf16[16,512,128]{2,1,0:T(8,128)(2,1)}, f32[4,8,128]{2,1,0:T(8,128)}) custom-call(s32[4,16,128]{2,1,0:T(8,128)} %get-tuple-element.13.lists.lists_v, s32[4,16,128]{2,1,0:T(8,128)} %get-tuple-element.13.lists.lists_v, f32[8,128]{1,0:T(8,128)} %get-tuple-element.14.weights, bf16[16,384,128]{2,1,0:T(8,128)(2,1)} %get-tuple-element.15.back), custom_call_target="tpu_custom_call" | custom-call | tf_op jit(solution)/shard_map/add_up/pallas_call | solution.py:606
  67.2 56.5 %wiener.1 = (bf16[512,512]{1,0:T(8,128)(2,1)}, bf16[16,384,128]{2,1,0:T(8,128)(2,1)}, f32[8,128]{1,0:T(8,128)}) custom-call(bf16[16,512,128]{2,1,0:T(8,128)(2,1)} %get-tuple-element.16.acc, f32[4,8,128]{2,1,0:T(8,128)} %get-tuple-element.17.wsum, bf16[512,512]{1,0:T(8,128)(2,1)} %noisy.3, bf16[512,512]{1,0:T(8,128)(2,1)} %constant.5.clone.cube, ...), custom_call_target="tpu_custom_call" | custom-call | tf_op jit(solution)/shard_map/wiener/pallas_call | solution.py:651
  123.7 19.7 %add_up.3 = (bf16[16,512,128]{2,1,0:T(8,128)(2,1)}, f32[4,8,128]{2,1,0:T(8,128)}) custom-call(s32[4,16,128]{2,1,0:T(8,128)} %get-tuple-element.13.lists.lists_v, s32[4,16,128]{2,1,0:T(8,128)} %get-tuple-element.13.lists.lists_v, f32[8,128]{1,0:T(8,128)} %get-tuple-element.20.weights, bf16[16,384,128]{2,1,0:T(8,128)(2,1)} %get-tuple-element.21.back), custom_call_target="tpu_custom_call" | custom-call | tf_op jit(solution)/shard_map/add_up/pallas_call | solution.py:606
  143.4 0.0 copy-start
  143.4 22.2 %settle.1 = bf16[512,512]{1,0:T(8,128)(2,1)} custom-call(bf16[16,512,128]{2,1,0:T(8,128)(2,1)} %get-tuple-element.22.acc, f32[4,8,128]{2,1,0:T(8,128)} %get-tuple-element.23.wsum, bf16[512,512]{1,0:T(8,128)(2,1)} %noisy.3, bf16[512,512]{1,0:T(8,128)(2,1)} %constant.5.clone.cube), custom_call_target="tpu_custom_call" | custom-call | tf_op jit(solution)/shard_map/settle/pallas_call | solution.py:667
  165.6 0.0 copy-done
  165.6 0.8 copy.10
  166.4 1.9 %copy.11 = bf16[512,512]{1,0:T(8,128)(2,1)} copy(bf16[512,512]{1,0:T(8,128)(2,1)} %settle.1) | data formatting | bytes 1048576
Async XLA Ops:
  143.4 22.2 %copy-start = (bf16[512,512]{1,0:T(8,128)(2,1)S(1)}, bf16[512,512]{1,0:T(8,128)(2,1)}, u32[]{:S(2)}) copy-start(bf16[512,512]{1,0:T(8,128)(2,1)} %get-tuple-element.26) | copy-start | bytes 1572868

commit v2 on v1

--- a/solution.py
+++ b/solution.py
@@ -1,4 +1,5 @@
 import functools
+import itertools
 
 import jax
 import jax.numpy as jnp
@@ -14,7 +15,6 @@
 SUBS = 8
 PIECES = 2
 STREAMS = 4
-TOGETHER = 2
 LIMIT = 60 * 1024 * 1024
 MESH = pl.DeviceIdType.MESH
 VMEM = pl.BlockSpec(memory_space=pltpu.VMEM)
@@ -75,11 +75,13 @@
 
 
 def flip(value, mask):
-    bit = 1
-    while bit <= mask:
-        if mask & bit:
-            value = value + bit - 2 * bit * lax.rem(value // bit, 2)
-        bit *= 2
+    if isinstance(mask, int):
+        for bit in (1 << b for b in range(mask.bit_length())):
+            if mask & bit:
+                value = value + bit - 2 * bit * lax.rem(value // bit, 2)
+        return value
+    for bit in (1, 2):
+        value = value + bit * lax.rem(mask // bit, 2) * (1 - 2 * lax.rem(value // bit, 2))
     return value
 
 
@@ -141,25 +143,25 @@
                 copy.start()
                 self.started.append(copy)
 
-    def begin(self, rows, cube_t):
+    def begin(self, h, rows, cube_t):
         place = self.place
-        for off in list(range(place.parts - 1, 0, -1)) + [0]:
+        for off in list(range(1, place.parts)) + [0]:
             columns = pl.ds(pl.multiple_of(flip(place.part, off) * LANES, LANES), LANES)
             spec = jnp.dot(rows, cube_t[:, columns], preferred_element_type=jnp.float32)
-            self.stage[off] = spec.astype(self.stage.dtype)
-            for h in range(PIECES):
-                if off == 0:
-                    self.pass_on(0, 0, h)
-                    continue
-                copy = remote(
-                    piece_of(self.stage.at[off], h),
-                    piece_of(self.got.at[off, 0], h),
-                    self.send.at[off, 0, h],
-                    self.recv.at[off, 0, h],
-                    place.device(off, 0),
-                )
-                copy.start()
-                self.started.append(copy)
+            piece = piece_of(self.stage.at[off], h)
+            piece[...] = spec.astype(self.stage.dtype)
+            if off == 0:
+                self.pass_on(0, 0, h)
+                continue
+            copy = remote(
+                piece,
+                piece_of(self.got.at[off, 0], h),
+                self.send.at[off, 0, h],
+                self.recv.at[off, 0, h],
+                place.device(off, 0),
+            )
+            copy.start()
+            self.started.append(copy)
 
     def widen(self, off, d, h):
         source = piece_of(self.block(off, d), h)
@@ -174,7 +176,7 @@
 
         def when(key):
             off, d, h = key
-            return (place.parts - off if off else 0) + 0.5 * h + sum(0.3 if b == 1 else 1.0 for b in place.bits if d & b)
+            return off + place.parts * h + sum(0.3 if b == 1 else 1.0 for b in place.bits if d & b)
 
         keys = [
             (off, d, h)
@@ -209,16 +211,27 @@
     ]
 
 
-def pick_rows(table, lists, members, some):
-    parts, group = lists.shape[:2]
-    for src in range(parts):
-
-        def step(q, carry):
+def pick_rows(table, lists, first, members, some):
+    group = members.shape[0]
+    each = LANES // group
+
+    def step(t, carry):
+        src, row = t // (some // each), lax.rem(t, some // each)
+        for q in range(each):
             for m in range(group):
-                members[m, pl.ds(src * some + q, 1), :] = table[pl.ds(lists[src, m, q], 1), :]
-            return carry
-
-        lax.fori_loop(0, some, step, 0, unroll=4)
+                spot = lists[src, first + row, q * group + m]
+                members[m, pl.ds(t * each + q, 1), :] = table[pl.ds(spot, 1), :]
+        return carry
+
+    lax.fori_loop(0, lists.shape[0] * some // each, step, 0)
+
+
+def find_equals(lists, same, group, some):
+    for src in range(lists.shape[0]):
+        rows = lists[src, :group, :]
+        equal = [jnp.where(rows == pltpu.roll(rows, back, 0), 1.0, 0.0) for back in range(1, group // STREAMS)]
+        equal.append(jnp.zeros((LANES - group * len(equal), LANES), jnp.float32))
+        same[src * some : (src + 1) * some, :] = jnp.concatenate(equal, axis=0).T[:some, :]
 
 
 def diagonal(rows):
@@ -226,7 +239,7 @@
     return lax.broadcasted_iota(jnp.int32, shape, 0) == lax.broadcasted_iota(jnp.int32, shape, 1)
 
 
-def shrink_groups(place, second, width, some, sigma, members, coeffs, back, energy, ebuf, egot, weights, send, recv):
+def shrink_groups(place, second, width, some, sigma, members, coeffs, back, same, energy, ebuf, egot, weights, send, recv, then=None):
     group, refs = members.shape[:2]
     factor = scales(group)
     columns = pl.ds(pl.multiple_of(place.part * LANES, LANES), LANES)
@@ -252,6 +265,8 @@
         return carry
 
     lax.fori_loop(0, refs // SUBS, forward, 0)
+    if then is not None:
+        then()
     parts = refs // some
     for src in range(parts):
         column = jnp.sum(energy[src * some : (src + 1) * some, :], axis=1, keepdims=True)
@@ -266,7 +281,11 @@
         rows = pl.ds(pl.multiple_of(b * 2 * SUBS, 2 * SUBS), 2 * SUBS)
         values = cosine_sums_transposed([members[j, rows, :] * factor[j] for j in range(group)])
         for m in range(group):
-            back[m, rows, :] = values[m].astype(back.dtype)
+            merged = values[m]
+            for before in range(1, m % (group // STREAMS) + 1):
+                lane = (before - 1) * group + m
+                merged = merged + same[rows, lane : lane + 1] * values[m - before]
+            back[m, rows, :] = merged.astype(back.dtype)
         return carry
 
     lax.fori_loop(0, refs // (2 * SUBS), inverse, 0)
@@ -284,6 +303,7 @@
     return [
         pltpu.VMEM((group, refs, LANES), jnp.float32),
         pltpu.VMEM((refs, LANES), jnp.float32),
+        pltpu.VMEM((refs, LANES), jnp.float32),
         pltpu.VMEM((SUBS, LANES), jnp.float32),
         pltpu.VMEM((parts, SUBS, LANES), jnp.float32),
         SEMS((parts,)),
@@ -291,25 +311,42 @@
     ]
 
 
-def first_kernel(count, x, home, ids, sigma, cube_t, coeffs, back, weights, lists_out, *scratch):
+def first_kernel(count, x, home, ids, sigma, cube_t, coeffs_out, back, weights, lists_out, *scratch):
     stage, got, table, send, recv = scratch[:5]
-    members, energy, ebuf, egot, esend, erecv = scratch[5:11]
-    named, lists_v, lists_s, lsend, lrecv, lsem = scratch[11:]
+    members, same, energy, ebuf, egot, esend, erecv = scratch[5:12]
+    coeffs, csem, named, lists_v, lists_s, lsend, lrecv, lsem = scratch[12:]
     parts = stage.shape[0]
     group, some = ids.shape
+    each = LANES // group
+    size = x.shape[0] // PIECES
     place = Place(count, parts)
     place.greet()
     spread = Spread(place, stage, got, table, send, recv)
-    spread.begin(x[...], cube_t)
-
-    def look_up(m, carry):
-        for q in range(some):
-            named[m, q] = home[ids[m, q]]
+    spread.begin(0, x[:size, :], cube_t)
+
+    def look_up(row, carry):
+        for q in range(each):
+            for m in range(group):
+                spot = home[ids[m, row * each + q]]
+                named[m, row * each + q] = spot
+                named[group + row, q * group + m] = spot
+        return carry
+
+    lax.fori_loop(0, some // each, look_up, 0)
+
+    def fill(m, carry):
         for q in range(some, LANES):
             named[m, q] = 0
         return carry
 
-    lax.fori_loop(0, group, look_up, 0)
+    lax.fori_loop(0, group, fill, 0)
+
+    def fill_rows(row, carry):
+        for q in range(LANES):
+            named[row, q] = 0
+        return carry
+
+    lax.fori_loop(group + some // each, named.shape[0], fill_rows, 0)
     ebuf[...] = jnp.zeros(ebuf.shape, ebuf.dtype)
     mine = pltpu.make_async_copy(named, lists_v.at[place.part], lsem.at[0])
     mine.start()
@@ -325,6 +362,8 @@
         )
         copy.start()
         started.append(copy)
+    for h in range(1, PIECES):
+        spread.begin(h, x[h * size : (h + 1) * size, :], cube_t)
     spread.finish()
     copies = []
     for off in range(parts):
@@ -334,13 +373,16 @@
         copy = pltpu.make_async_copy(source, lists_s.at[flip(place.part, off)], lsem.at[off])
         copy.start()
         copies.append(copy)
+    lists_out[...] = lists_v[...]
+    find_equals(lists_v, same, group, some)
     for copy in copies:
         copy.wait()
-    lists_out[...] = lists_v[...]
-    pick_rows(table, lists_s, members, some)
+    pick_rows(table, lists_s, group, members, some)
+    store = pltpu.make_async_copy(coeffs, coeffs_out, csem.at[0])
     shrink_groups(
-        place, False, x.shape[1], some, sigma, members, coeffs, back, energy, ebuf, egot, weights, esend, erecv
+        place, False, x.shape[1], some, sigma, members, coeffs, back, same, energy, ebuf, egot, weights, esend, erecv, store.start
     )
+    store.wait()
     for copy in started:
         copy.wait_send()
     spread.close()
@@ -350,7 +392,9 @@
     def __init__(self, place, acc, own, got, sent, zgot, local, send, recv):
         self.place, self.acc, self.own, self.got, self.sent, self.zgot = place, acc, own, got, sent, zgot
         self.local, self.send, self.recv, self.started = local, send, recv, []
-        self.order = list(range(place.parts - 1, -1, -1))
+        last = place.parts - 1
+        inner = jnp.where((place.part == 0) | (place.part == last), 0, 1)
+        self.order = [inner * (i + 1) + (1 - inner) * (last - i) for i in range(last)] + [0]
 
     def start(self, copy):
         copy.start()
@@ -369,9 +413,9 @@
 
     def begin(self):
         place = self.place
-        for d in sorted(range(1, place.ranks, 2), key=lambda d: lowest(d - 1, place.ranks)):
-            for off in self.order:
-                for h in range(PIECES):
+        for h in range(PIECES):
+            for d in sorted(range(1, place.ranks, 2), key=lambda d: lowest(d - 1, place.ranks)):
+                for off in self.order:
                     self.start(
                         remote(
                             piece_of(self.acc.at[place.index(off, d)], h),
@@ -398,12 +442,13 @@
 
     def run(self):
         place = self.place
-        for d in sorted(range(0, place.ranks, 2), key=lambda d: lowest(d, place.ranks)):
-            for off in self.order:
-                for h in range(PIECES):
+        for level in place.bits[1:] + [place.ranks]:
+            ds = [d for d in range(0, place.ranks, 2) if lowest(d, place.ranks) == level]
+            for h, d, i in itertools.product(range(PIECES), ds, range(place.parts)):
+                    off = self.order[i]
                     piece = piece_of(self.sent.at[off, d // 2], h)
                     piece[...] = self.value(off, d, h).astype(self.sent.dtype)
-                    if d == 0 and off == 0:
+                    if d == 0 and i == place.parts - 1:
                         continue
                     bit = lowest(d, 0)
                     self.start(
@@ -419,7 +464,7 @@
     def slices(self, h):
         place = self.place
         yield 0, piece_of(self.sent.at[0, 0], h)[...]
-        for off in self.order[:-1]:
+        for off in range(1, place.parts):
             piece = piece_of(self.zgot.at[off], h)
             remote(
                 piece, piece, self.send.at[off, 0, h], self.recv.at[off, 0, h], place.device(off, 0)
@@ -431,7 +476,7 @@
             copy.wait_send()
 
 
-def settle(place, acc, wsum, noisy, cube, out, own, got, sent, zgot, wgot, local, send, recv, wsend, wrecv):
+def settle(place, acc, wsum, noisy, cube, out, own, got, sent, zgot, wgot, local, send, recv, wsend, wrecv, then=None):
     held = noisy.shape[0]
     collect = Collect(place, acc, own, got, sent, zgot, local, send, recv)
     collect.open()
@@ -459,6 +504,8 @@
             out[pl.ds(row * LANES, LANES), :] = (
                 numer[j * LANES : (j + 1) * LANES, :] / (column + prior_weight)
             ).astype(out.dtype)
+        if then is not None:
+            then(h)
     return collect
 
 
@@ -479,23 +526,34 @@
     ]
 
 
-def second_kernel(count, some, acc, wsum, noisy, cube, cube_t, sigma, lists, coeffs_in, basic, back, weights, *scratch):
+def second_kernel(count, some, acc, wsum, noisy, cube, cube_t, sigma, lists, lists_v, coeffs_in, basic, back, weights, *scratch):
     stage, got, table, send, recv = scratch[:5]
-    members, energy, ebuf, egot, esend, erecv = scratch[5:11]
-    coeffs, csem = scratch[11:13]
+    members, same, energy, ebuf, egot, esend, erecv = scratch[5:12]
+    coeffs, csem = scratch[12:14]
+    group = members.shape[0]
+    size = noisy.shape[0] // PIECES
     parts = stage.shape[0]
     place = Place(count, parts)
     fetch = pltpu.make_async_copy(coeffs_in, coeffs, csem.at[0])
     fetch.start()
-    collect = settle(place, acc, wsum, noisy, cube, basic, *scratch[13:])
     spread = Spread(place, stage, got, table, send, recv)
-    spread.begin(basic[...], cube_t)
     ebuf[...] = jnp.zeros(ebuf.shape, ebuf.dtype)
+    find_equals(lists_v, same, group, some)
+    collect = settle(
+        place,
+        acc,
+        wsum,
+        noisy,
+        cube,
+        basic,
+        *scratch[14:],
+        then=lambda h: spread.begin(h, basic[h * size : (h + 1) * size, :], cube_t),
+    )
     spread.finish()
-    pick_rows(table, lists, members, some)
+    pick_rows(table, lists, group, members, some)
     fetch.wait()
     shrink_groups(
-        place, True, noisy.shape[1], some, sigma, members, coeffs, back, energy, ebuf, egot, weights, esend, erecv
+        place, True, noisy.shape[1], some, sigma, members, coeffs, back, same, energy, ebuf, egot, weights, esend, erecv
     )
     collect.close()
     spread.close()
@@ -506,7 +564,8 @@
 
 
 def add_kernel(count, some, lists, lists_v, weights, back, acc, wsum, members, *sums):
-    parts, group = lists.shape[:2]
+    parts, group = lists.shape[0], members.shape[0]
+    each = LANES // group
     place = Place(count, parts)
     blocks, held = acc.shape[:2]
 
@@ -549,34 +608,28 @@
             preferred_element_type=jnp.float32,
         )
 
-    total = lax.fori_loop(0, group, weigh, jnp.zeros((many, LANES), jnp.float32))
+    total = lax.fori_loop(0, group, weigh, jnp.zeros((many, LANES), jnp.float32), unroll=True)
     per = held // LANES
     for b in range(wsum.shape[0]):
         wsum[b, :per, :] = total[b * per : (b + 1) * per, :]
         if per < SUBS:
             wsum[b, per:, :] = jnp.zeros((SUBS - per, LANES), jnp.float32)
 
-    for src in range(parts):
-
-        def step(q, carry):
-            for base in range(0, group, STREAMS * TOGETHER):
-                spots, news = [], []
-                for s in range(STREAMS):
-                    ms = [base + s * TOGETHER + t for t in range(TOGETHER)]
-                    where = [lists[src, m, q] for m in ms]
-                    extra = [members[m, pl.ds(src * some + q, 1), :] for m in ms]
-                    fresh = [sums[s][pl.ds(w, 1), :] + e for w, e in zip(where, extra)]
-                    for t in range(TOGETHER):
-                        for u in range(t):
-                            fresh[t] = fresh[t] + jnp.where(where[u] == where[t], extra[u], 0.0)
-                    spots.append(where)
-                    news.append(fresh)
-                for s in range(STREAMS):
-                    for w, n in zip(spots[s], news[s]):
-                        sums[s][pl.ds(w, 1), :] = n
-            return carry
-
-        lax.fori_loop(0, some, step, 0, unroll=2)
+    together = group // STREAMS
+
+    def step(t, carry):
+        src, row = t // (some // each), lax.rem(t, some // each)
+        for q in range(each):
+            spots, news = [], []
+            for m in range(group):
+                spot = lists[src, group + row, q * group + m]
+                spots.append(spot)
+                news.append(sums[m // together][pl.ds(spot, 1), :] + members[m, pl.ds(t * each + q, 1), :])
+            for m in range(group):
+                sums[m // together][pl.ds(spots[m], 1), :] = news[m]
+        return carry
+
+    lax.fori_loop(0, parts * some // each, step, 0)
 
     def store(b, carry):
         for i in range(held // LANES):
@@ -601,7 +654,7 @@
 
 
 def add_up(count, some, held, lists, weights, back):
-    parts, group = lists.shape[:2]
+    parts, group = lists.shape[0], back.shape[0]
     ranks = count // parts
     return pl.pallas_call(
         functools.partial(add_kernel, count, some),
@@ -631,15 +684,17 @@
             shape(group, refs, LANES),
             shape(group, refs, LANES, dtype=dtype),
             shape(SUBS, LANES),
-            shape(parts, group, LANES, dtype=jnp.int32),
+            shape(parts, 2 * group, LANES, dtype=jnp.int32),
         ],
         in_specs=[VMEM, SMEM, SMEM, VMEM, VMEM],
-        out_specs=[VMEM] * 4,
+        out_specs=[HBM] + [VMEM] * 3,
         scratch_shapes=shared
         + [
-            pltpu.SMEM((group, LANES), jnp.int32),
-            pltpu.VMEM((parts, group, LANES), jnp.int32),
-            pltpu.SMEM((parts, group, LANES), jnp.int32),
+            pltpu.VMEM((group, refs, LANES), jnp.float32),
+            SEMS((1,)),
+            pltpu.SMEM((2 * group, LANES), jnp.int32),
+            pltpu.VMEM((parts, 2 * group, LANES), jnp.int32),
+            pltpu.SMEM((parts, 2 * group, LANES), jnp.int32),
             SEMS((parts,)),
             SEMS((parts,)),
             SEMS((parts,)),
@@ -655,14 +710,14 @@
             shape(group, refs, LANES, dtype=dtype),
             shape(SUBS, LANES),
         ],
-        in_specs=[HBM] + [VMEM] * 5 + [SMEM, HBM],
+        in_specs=[HBM] + [VMEM] * 5 + [SMEM, VMEM, HBM],
         out_specs=[VMEM] * 3,
         scratch_shapes=shared
         + [pltpu.VMEM((group, refs, LANES), jnp.float32), SEMS((1,))]
         + settle_scratch(count, parts, held, dtype),
         compiler_params=params(1),
         name="wiener",
-    )(acc, wsum, noisy, cube, cube_t, sigma, lists, coeffs)
+    )(acc, wsum, noisy, cube, cube_t, sigma, lists, lists, coeffs)
     acc, wsum = add_up(count, some, held, lists, weights, back)
     final = pl.pallas_call(
         functools.partial(third_kernel, count, parts),

time: 169 us -> 163 us (0.964)
  Pallas kernels: 165 us -> 160 us
    pallas_call x2, Pallas kernels: 39.5 us -> 24.6 us  [add_up(): pl.pallas_call(functools.partial(add_kernel, count, some), out_shape=[sha...]
    pallas_call x1, Pallas kernels: 56.5 us -> 61.6 us  [body(): pl.pallas_call(functools.partial(second_kernel, count, some), out_shape=[...]
    pallas_call x1, Pallas kernels: 46.8 us -> 50 us  [body(): pl.pallas_call(functools.partial(first_kernel, count), out_shape=[shape(g...]
where the time goes in v2:
time: 163 us
  Pallas kernels  160 us (98%)
  local copies, waits for them, and re-layouts  2.67 us (2%)
    pallas_call x1, Pallas kernels, body(): pl.pallas_call(functools.partial(second_kernel, count, some), out_shape=[...  61.6 us
    pallas_call x1, Pallas kernels, body(): pl.pallas_call(functools.partial(first_kernel, count), out_shape=[shape(g...  50 us
    pallas_call x2, Pallas kernels, add_up(): pl.pallas_call(functools.partial(add_kernel, count, some), out_shape=[sha...  24.6 us
    pallas_call x1, Pallas kernels, body(): pl.pallas_call(functools.partial(third_kernel, count, parts), out_shape=s...  23.3 us

profile of v2, /device:TPU:0, one launch (start us, length us, event | category | flops | bytes accessed | tf_op | source)
XLA Modules:
  0.0 162.9 jit_solution(7586976601077177876)
XLA Ops:
  0.6 50.0 %shrink.1 = (f32[16,384,128]{2,1,0:T(8,128)}, bf16[16,384,128]{2,1,0:T(8,128)(2,1)}, f32[8,128]{1,0:T(8,128)}, s32[4,32,128]{2,1,0:T(8,128)}) custom-call(bf16[512,512]{1,0:T(8,128)(2,1)} %noisy.3, s32[8192]{0:T(1024)} %home.1, s32[16,96]{1,0:T(8,128)} %bitcast.4, f32[1,512]{1,0:T(1,128)} %bitcast.2, bf16[512,512]{1,0:T(8,128)(2,1)} %constant.4.clone.cube_t), custom_call_target="tpu_custom_call" | custom-call | tf_op jit(solution)/shard_map/shrink/pallas_call | solution.py:681
  50.7 12.3 %add_up.2 = (bf16[16,512,128]{2,1,0:T(8,128)(2,1)}, f32[4,8,128]{2,1,0:T(8,128)}) custom-call(s32[4,32,128]{2,1,0:T(8,128)} %get-tuple-element.13.lists.lists_v, s32[4,32,128]{2,1,0:T(8,128)} %get-tuple-element.13.lists.lists_v, f32[8,128]{1,0:T(8,128)} %get-tuple-element.14.weights, bf16[16,384,128]{2,1,0:T(8,128)(2,1)} %get-tuple-element.15.back), custom_call_target="tpu_custom_call" | custom-call | tf_op jit(solution)/shard_map/add_up/pallas_call | solution.py:659
  63.0 61.6 %wiener.1 = (bf16[512,512]{1,0:T(8,128)(2,1)}, bf16[16,384,128]{2,1,0:T(8,128)(2,1)}, f32[8,128]{1,0:T(8,128)}) custom-call(bf16[16,512,128]{2,1,0:T(8,128)(2,1)} %get-tuple-element.16.acc, f32[4,8,128]{2,1,0:T(8,128)} %get-tuple-element.17.wsum, bf16[512,512]{1,0:T(8,128)(2,1)} %noisy.3, bf16[512,512]{1,0:T(8,128)(2,1)} %constant.5.clone.cube, ...), custom_call_target="tpu_custom_call" | custom-call | tf_op jit(solution)/shard_map/wiener/pallas_call | solution.py:706
  124.6 12.3 %add_up.3 = (bf16[16,512,128]{2,1,0:T(8,128)(2,1)}, f32[4,8,128]{2,1,0:T(8,128)}) custom-call(s32[4,32,128]{2,1,0:T(8,128)} %get-tuple-element.13.lists.lists_v, s32[4,32,128]{2,1,0:T(8,128)} %get-tuple-element.13.lists.lists_v, f32[8,128]{1,0:T(8,128)} %get-tuple-element.20.weights, bf16[16,384,128]{2,1,0:T(8,128)(2,1)} %get-tuple-element.21.back), custom_call_target="tpu_custom_call" | custom-call | tf_op jit(solution)/shard_map/add_up/pallas_call | solution.py:659
  136.9 0.0 copy-start
  136.9 23.3 %settle.1 = bf16[512,512]{1,0:T(8,128)(2,1)} custom-call(bf16[16,512,128]{2,1,0:T(8,128)(2,1)} %get-tuple-element.22.acc, f32[4,8,128]{2,1,0:T(8,128)} %get-tuple-element.23.wsum, bf16[512,512]{1,0:T(8,128)(2,1)} %noisy.3, bf16[512,512]{1,0:T(8,128)(2,1)} %constant.5.clone.cube), custom_call_target="tpu_custom_call" | custom-call | tf_op jit(solution)/shard_map/settle/pallas_call | solution.py:722
  160.3 0.0 copy-done
  160.3 0.8 copy.10
  161.1 1.9 %copy.11 = bf16[512,512]{1,0:T(8,128)(2,1)} copy(bf16[512,512]{1,0:T(8,128)(2,1)} %settle.1) | data formatting | bytes 1048576
Async XLA Ops:
  136.9 23.3 %copy-start = (bf16[512,512]{1,0:T(8,128)(2,1)S(1)}, bf16[512,512]{1,0:T(8,128)(2,1)}, u32[]{:S(2)}) copy-start(bf16[512,512]{1,0:T(8,128)(2,1)} %get-tuple-element.26) | copy-start | bytes 1572868

commit v3 on v2

--- a/solution.py
+++ b/solution.py
@@ -15,7 +15,6 @@
 SUBS = 8
 PIECES = 2
 STREAMS = 4
-LIMIT = 60 * 1024 * 1024
 MESH = pl.DeviceIdType.MESH
 VMEM = pl.BlockSpec(memory_space=pltpu.VMEM)
 SMEM = pl.BlockSpec(memory_space=pltpu.SMEM)
@@ -176,7 +175,7 @@
 
         def when(key):
             off, d, h = key
-            return off + place.parts * h + sum(0.3 if b == 1 else 1.0 for b in place.bits if d & b)
+            return off + 0.5 * h + sum(2.2 if b == 1 else 1.6 for b in place.bits if d & b)
 
         keys = [
             (off, d, h)
@@ -239,7 +238,7 @@
     return lax.broadcasted_iota(jnp.int32, shape, 0) == lax.broadcasted_iota(jnp.int32, shape, 1)
 
 
-def shrink_groups(place, second, width, some, sigma, members, coeffs, back, same, energy, ebuf, egot, weights, send, recv, then=None):
+def shrink_groups(place, second, width, some, sigma, members, coeffs, back, lists_v, same, energy, ebuf, egot, weights, send, recv, then=None):
     group, refs = members.shape[:2]
     factor = scales(group)
     columns = pl.ds(pl.multiple_of(place.part * LANES, LANES), LANES)
@@ -277,6 +276,8 @@
         copy.start()
         started.append(copy)
 
+    find_equals(lists_v, same, group, some)
+
     def inverse(b, carry):
         rows = pl.ds(pl.multiple_of(b * 2 * SUBS, 2 * SUBS), 2 * SUBS)
         values = cosine_sums_transposed([members[j, rows, :] * factor[j] for j in range(group)])
@@ -311,18 +312,26 @@
     ]
 
 
-def first_kernel(count, x, home, ids, sigma, cube_t, coeffs_out, back, weights, lists_out, *scratch):
+def first_kernel(count, x_in, home_in, ids_in, sigma_in, cube_in, coeffs_out, back, weights, lists_out, *scratch):
     stage, got, table, send, recv = scratch[:5]
     members, same, energy, ebuf, egot, esend, erecv = scratch[5:12]
-    coeffs, csem, named, lists_v, lists_s, lsend, lrecv, lsem = scratch[12:]
+    x, cube_t, sigma, ids, insem = scratch[12:17]
+    coeffs, csem, home, named, lists_v, lists_s, lsend, lrecv, lsem = scratch[17:]
     parts = stage.shape[0]
     group, some = ids.shape
     each = LANES // group
     size = x.shape[0] // PIECES
     place = Place(count, parts)
+    pairs = [(x_in, x), (cube_in, cube_t), (home_in, home), (ids_in, ids), (sigma_in, sigma)]
+    fetches = [pltpu.make_async_copy(src, dst, insem.at[i]) for i, (src, dst) in enumerate(pairs)]
+    for fetch in fetches:
+        fetch.start()
     place.greet()
+    for fetch in fetches[:2]:
+        fetch.wait()
     spread = Spread(place, stage, got, table, send, recv)
-    spread.begin(0, x[:size, :], cube_t)
+    for h in range(PIECES):
+        spread.begin(h, x[h * size : (h + 1) * size, :], cube_t)
 
     def look_up(row, carry):
         for q in range(each):
@@ -332,6 +341,8 @@
                 named[group + row, q * group + m] = spot
         return carry
 
+    for fetch in fetches[2:]:
+        fetch.wait()
     lax.fori_loop(0, some // each, look_up, 0)
 
     def fill(m, carry):
@@ -362,8 +373,6 @@
         )
         copy.start()
         started.append(copy)
-    for h in range(1, PIECES):
-        spread.begin(h, x[h * size : (h + 1) * size, :], cube_t)
     spread.finish()
     copies = []
     for off in range(parts):
@@ -374,13 +383,12 @@
         copy.start()
         copies.append(copy)
     lists_out[...] = lists_v[...]
-    find_equals(lists_v, same, group, some)
     for copy in copies:
         copy.wait()
     pick_rows(table, lists_s, group, members, some)
     store = pltpu.make_async_copy(coeffs, coeffs_out, csem.at[0])
     shrink_groups(
-        place, False, x.shape[1], some, sigma, members, coeffs, back, same, energy, ebuf, egot, weights, esend, erecv, store.start
+        place, False, x.shape[1], some, sigma, members, coeffs, back, lists_v, same, energy, ebuf, egot, weights, esend, erecv, store.start
     )
     store.wait()
     for copy in started:
@@ -538,7 +546,6 @@
     fetch.start()
     spread = Spread(place, stage, got, table, send, recv)
     ebuf[...] = jnp.zeros(ebuf.shape, ebuf.dtype)
-    find_equals(lists_v, same, group, some)
     collect = settle(
         place,
         acc,
@@ -553,7 +560,7 @@
     pick_rows(table, lists, group, members, some)
     fetch.wait()
     shrink_groups(
-        place, True, noisy.shape[1], some, sigma, members, coeffs, back, same, energy, ebuf, egot, weights, esend, erecv
+        place, True, noisy.shape[1], some, sigma, members, coeffs, back, lists_v, same, energy, ebuf, egot, weights, esend, erecv
     )
     collect.close()
     spread.close()
@@ -647,9 +654,10 @@
     return jax.ShapeDtypeStruct(dims, dtype)
 
 
-def params(collective_id=None):
+def params(rows, collective_id=None):
+    limit = 5 * rows * LANES * 4 + (10 << 20)
     return pltpu.CompilerParams(
-        collective_id=collective_id, has_side_effects=collective_id is not None, vmem_limit_bytes=LIMIT
+        collective_id=collective_id, has_side_effects=collective_id is not None, vmem_limit_bytes=limit
     )
 
 
@@ -663,7 +671,7 @@
         out_specs=[VMEM, VMEM],
         scratch_shapes=[pltpu.VMEM((group, parts * some, LANES), jnp.float32)]
         + [pltpu.VMEM((count * held, LANES), jnp.float32)] * STREAMS,
-        compiler_params=params(),
+        compiler_params=params(count * held),
         name="add_up",
     )(lists, lists, weights, back)
 
@@ -686,12 +694,18 @@
             shape(SUBS, LANES),
             shape(parts, 2 * group, LANES, dtype=jnp.int32),
         ],
-        in_specs=[VMEM, SMEM, SMEM, VMEM, VMEM],
+        in_specs=[HBM] * 5,
         out_specs=[HBM] + [VMEM] * 3,
         scratch_shapes=shared
         + [
+            pltpu.VMEM(noisy.shape, dtype),
+            pltpu.VMEM(cube_t.shape, dtype),
+            pltpu.VMEM(sigma.shape, jnp.float32),
+            pltpu.SMEM((group, some), jnp.int32),
+            SEMS((5,)),
             pltpu.VMEM((group, refs, LANES), jnp.float32),
             SEMS((1,)),
+            pltpu.SMEM(cube_home.shape, jnp.int32),
             pltpu.SMEM((2 * group, LANES), jnp.int32),
             pltpu.VMEM((parts, 2 * group, LANES), jnp.int32),
             pltpu.SMEM((parts, 2 * group, LANES), jnp.int32),
@@ -699,9 +713,9 @@
             SEMS((parts,)),
             SEMS((parts,)),
         ],
-        compiler_params=params(0),
+        compiler_params=params(count * held, 0),
         name="shrink",
-    )(noisy, cube_home, matches.T, sigma, cube_t)
+    )(*[pltpu.with_memory_space_constraint(v, pltpu.HBM) for v in (noisy, cube_home, matches.T, sigma, jnp.asarray(cube_t))])
     acc, wsum = add_up(count, some, held, lists, weights, back)
     basic, back, weights = pl.pallas_call(
         functools.partial(second_kernel, count, some),
@@ -715,7 +729,7 @@
         scratch_shapes=shared
         + [pltpu.VMEM((group, refs, LANES), jnp.float32), SEMS((1,))]
         + settle_scratch(count, parts, held, dtype),
-        compiler_params=params(1),
+        compiler_params=params(count * held, 1),
         name="wiener",
     )(acc, wsum, noisy, cube, cube_t, sigma, lists, lists, coeffs)
     acc, wsum = add_up(count, some, held, lists, weights, back)
@@ -725,7 +739,7 @@
         in_specs=[HBM] + [VMEM] * 3,
         out_specs=VMEM,
         scratch_shapes=settle_scratch(count, parts, held, dtype),
-        compiler_params=params(2),
+        compiler_params=params(count * held, 2),
         name="settle",
     )(acc, wsum, noisy, cube)
     return basic, final

time: 163 us -> 135 us (0.83)
  Pallas kernels: 160 us -> 133 us
    pallas_call x1, Pallas kernels: 50 us -> 38.2 us  [body(): pl.pallas_call(functools.partial(first_kernel, count), out_shape=[shape(g...]
    pallas_call x1, Pallas kernels: 61.6 us -> 51.7 us  [body(): pl.pallas_call(functools.partial(second_kernel, count, some), out_shape=[...]
    pallas_call x2, Pallas kernels: 24.6 us -> 21.4 us  [add_up(): pl.pallas_call(functools.partial(add_kernel, count, some), out_shape=[sha...]
    pallas_call x1, Pallas kernels: 23.3 us -> 21.6 us  [body(): pl.pallas_call(functools.partial(third_kernel, count, parts), out_shape=s...]
where the time goes in v3:
time: 135 us
  Pallas kernels  133 us (99%)
  local copies, waits for them, and re-layouts  1.61 us (1%)
    pallas_call x1, Pallas kernels, body(): pl.pallas_call(functools.partial(second_kernel, count, some), out_shape=[...  51.7 us
    pallas_call x1, Pallas kernels, body(): pl.pallas_call(functools.partial(first_kernel, count), out_shape=[shape(g...  38.2 us
    pallas_call x1, Pallas kernels, body(): pl.pallas_call(functools.partial(third_kernel, count, parts), out_shape=s...  21.6 us
    pallas_call x2, Pallas kernels, add_up(): pl.pallas_call(functools.partial(add_kernel, count, some), out_shape=[sha...  21.4 us

profile of v3, /device:TPU:0, one launch (start us, length us, event | category | flops | bytes accessed | tf_op | source)
XLA Modules:
  0.0 135.3 jit_solution(1446215239519419786)
XLA Ops:
  0.6 0.0 copy-start.2
  0.6 0.0 copy-start.1
  0.7 0.0 copy-start
  0.7 0.0 copy-start.3
  0.7 38.2 %shrink.1 = (f32[16,384,128]{2,1,0:T(8,128)S(1)}, bf16[16,384,128]{2,1,0:T(8,128)(2,1)S(1)}, f32[8,128]{1,0:T(8,128)S(1)}, s32[4,32,128]{2,1,0:T(8,128)S(1)}) custom-call(bf16[512,512]{1,0:T(8,128)(2,1)} %noisy.3, s32[8192]{0:T(1024)} %home_in.1, s32[16,96]{1,0:T(8,128)} %bitcast.4, f32[1,512]{1,0:T(1,128)} %bitcast.2, ...), custom_call_target="tpu_custom_call" | custom-call | tf_op jit(solution)/shard_map/shrink/pallas_call | solution.py:689
  38.9 10.7 %add_up.2 = (bf16[16,512,128]{2,1,0:T(8,128)(2,1)S(1)}, f32[4,8,128]{2,1,0:T(8,128)S(1)}) custom-call(s32[4,32,128]{2,1,0:T(8,128)S(1)} %get-tuple-element.13.lists.lists_v, s32[4,32,128]{2,1,0:T(8,128)S(1)} %get-tuple-element.13.lists.lists_v, f32[8,128]{1,0:T(8,128)S(1)} %get-tuple-element.14.weights, bf16[16,384,128]{2,1,0:T(8,128)(2,1)S(1)} %get-tuple-element.15.back), custom_call_target="tpu_custom_call" | custom-call | tf_op jit(solution)/shard_map/add_up/pallas_call | solution.py:667
  49.6 0.0 copy-done.2
  49.6 0.0 copy-done.1
  49.6 0.0 copy-done
  49.6 0.0 copy-done.3
  49.6 51.7 %wiener.1 = (bf16[512,512]{1,0:T(8,128)(2,1)S(1)}, bf16[16,384,128]{2,1,0:T(8,128)(2,1)S(1)}, f32[8,128]{1,0:T(8,128)S(1)}) custom-call(bf16[16,512,128]{2,1,0:T(8,128)(2,1)S(1)} %get-tuple-element.16.acc, f32[4,8,128]{2,1,0:T(8,128)S(1)} %get-tuple-element.17.wsum, bf16[512,512]{1,0:T(8,128)(2,1)S(1)} %copy-done, bf16[512,512]{1,0:T(8,128)(2,1)S(1)} %copy-done.1, ...), custom_call_target="tpu_custom_call" | custom-call | tf_op jit(solution)/shard_map/wiener/pallas_call | solution.py:720
  101.4 10.7 %add_up.3 = (bf16[16,512,128]{2,1,0:T(8,128)(2,1)S(1)}, f32[4,8,128]{2,1,0:T(8,128)S(1)}) custom-call(s32[4,32,128]{2,1,0:T(8,128)S(1)} %get-tuple-element.13.lists.lists_v, s32[4,32,128]{2,1,0:T(8,128)S(1)} %get-tuple-element.13.lists.lists_v, f32[8,128]{1,0:T(8,128)S(1)} %get-tuple-element.20.weights, bf16[16,384,128]{2,1,0:T(8,128)(2,1)S(1)} %get-tuple-element.21.back), custom_call_target="tpu_custom_call" | custom-call | tf_op jit(solution)/shard_map/add_up/pallas_call | solution.py:667
  112.1 21.6 %settle.1 = bf16[512,512]{1,0:T(8,128)(2,1)S(1)} custom-call(bf16[16,512,128]{2,1,0:T(8,128)(2,1)S(1)} %get-tuple-element.22.acc, f32[4,8,128]{2,1,0:T(8,128)S(1)} %get-tuple-element.23.wsum, bf16[512,512]{1,0:T(8,128)(2,1)S(1)} %copy-done, bf16[512,512]{1,0:T(8,128)(2,1)S(1)} %copy-done.1), custom_call_target="tpu_custom_call" | custom-call | tf_op jit(solution)/shard_map/settle/pallas_call | solution.py:736
  133.7 0.8 copy.10
  134.5 0.8 copy.11
Async XLA Ops:
  0.6 49.0 %copy-start.2 = (bf16[512,512]{1,0:T(8,128)(2,1)S(1)}, bf16[512,512]{1,0:T(8,128)(2,1)}, u32[]{:S(2)}) copy-start(bf16[512,512]{1,0:T(8,128)(2,1)} %constant.4.clone.cube_in.cube_t) | copy-start | bytes 1572868
  0.6 49.0 %copy-start.1 = (bf16[512,512]{1,0:T(8,128)(2,1)S(1)}, bf16[512,512]{1,0:T(8,128)(2,1)}, u32[]{:S(2)}) copy-start(bf16[512,512]{1,0:T(8,128)(2,1)} %constant.5.clone.cube) | copy-start | bytes 1572868
  0.7 49.0 %copy-start = (bf16[512,512]{1,0:T(8,128)(2,1)S(1)}, bf16[512,512]{1,0:T(8,128)(2,1)}, u32[]{:S(2)}) copy-start(bf16[512,512]{1,0:T(8,128)(2,1)} %noisy.3) | copy-start | bytes 1572868
  0.7 49.0 %copy-start.3 = (f32[512]{0:T(512)S(1)}, f32[512]{0:T(512)}, u32[]{:S(2)}) copy-start(f32[512]{0:T(512)} %param.9) | copy-start | bytes 6148

commit v4 on v3

--- a/solution.py
+++ b/solution.py
@@ -210,24 +210,30 @@
     ]
 
 
-def pick_rows(table, lists, first, members, some):
+def pick_rows(table, lists, members, some):
     group = members.shape[0]
-    each = LANES // group
 
     def step(t, carry):
-        src, row = t // (some // each), lax.rem(t, some // each)
-        for q in range(each):
+        src, row = t // (some // SUBS), lax.rem(t, some // SUBS)
+        for q in range(SUBS):
             for m in range(group):
-                spot = lists[src, first + row, q * group + m]
-                members[m, pl.ds(t * each + q, 1), :] = table[pl.ds(spot, 1), :]
+                spot = lists[m][src, row * SUBS + q]
+                members[m, pl.ds(t * SUBS + q, 1), :] = table[pl.ds(spot, 1), :]
         return carry
 
-    lax.fori_loop(0, lists.shape[0] * some // each, step, 0)
+    lax.fori_loop(0, members.shape[1] // SUBS, step, 0)
+
+
+def to_scalars(lists, scalars, sem):
+    copies = [pltpu.make_async_copy(lists.at[m], each, sem.at[m]) for m, each in enumerate(scalars)]
+    for copy in copies:
+        copy.start()
+    return copies
 
 
 def find_equals(lists, same, group, some):
     for src in range(lists.shape[0]):
-        rows = lists[src, :group, :]
+        rows = lists[src]
         equal = [jnp.where(rows == pltpu.roll(rows, back, 0), 1.0, 0.0) for back in range(1, group // STREAMS)]
         equal.append(jnp.zeros((LANES - group * len(equal), LANES), jnp.float32))
         same[src * some : (src + 1) * some, :] = jnp.concatenate(equal, axis=0).T[:some, :]
@@ -312,14 +318,14 @@
     ]
 
 
-def first_kernel(count, x_in, home_in, ids_in, sigma_in, cube_in, coeffs_out, back, weights, lists_out, *scratch):
+def first_kernel(count, x_in, home_in, ids_in, sigma_in, cube_in, coeffs_out, back, weights, lists_out, turned, *scratch):
     stage, got, table, send, recv = scratch[:5]
     members, same, energy, ebuf, egot, esend, erecv = scratch[5:12]
     x, cube_t, sigma, ids, insem = scratch[12:17]
-    coeffs, csem, home, named, lists_v, lists_s, lsend, lrecv, lsem = scratch[17:]
+    coeffs, csem, home, named, lists_v, lsend, lrecv, lsem = scratch[17:25]
+    scalars = scratch[25:]
     parts = stage.shape[0]
     group, some = ids.shape
-    each = LANES // group
     size = x.shape[0] // PIECES
     place = Place(count, parts)
     pairs = [(x_in, x), (cube_in, cube_t), (home_in, home), (ids_in, ids), (sigma_in, sigma)]
@@ -334,16 +340,14 @@
         spread.begin(h, x[h * size : (h + 1) * size, :], cube_t)
 
     def look_up(row, carry):
-        for q in range(each):
+        for q in range(SUBS):
             for m in range(group):
-                spot = home[ids[m, row * each + q]]
-                named[m, row * each + q] = spot
-                named[group + row, q * group + m] = spot
+                named[m, row * SUBS + q] = home[ids[m, row * SUBS + q]]
         return carry
 
     for fetch in fetches[2:]:
         fetch.wait()
-    lax.fori_loop(0, some // each, look_up, 0)
+    lax.fori_loop(0, some // SUBS, look_up, 0)
 
     def fill(m, carry):
         for q in range(some, LANES):
@@ -352,12 +356,6 @@
 
     lax.fori_loop(0, group, fill, 0)
 
-    def fill_rows(row, carry):
-        for q in range(LANES):
-            named[row, q] = 0
-        return carry
-
-    lax.fori_loop(group + some // each, named.shape[0], fill_rows, 0)
     ebuf[...] = jnp.zeros(ebuf.shape, ebuf.dtype)
     mine = pltpu.make_async_copy(named, lists_v.at[place.part], lsem.at[0])
     mine.start()
@@ -374,18 +372,17 @@
         copy.start()
         started.append(copy)
     spread.finish()
-    copies = []
-    for off in range(parts):
+    for off in range(1, parts):
         source = lists_v.at[flip(place.part, off)]
-        if off:
-            remote(source, source, lsend.at[off], lrecv.at[off], place.device(off, 0)).wait_recv()
-        copy = pltpu.make_async_copy(source, lists_s.at[flip(place.part, off)], lsem.at[off])
-        copy.start()
-        copies.append(copy)
+        remote(source, source, lsend.at[off], lrecv.at[off], place.device(off, 0)).wait_recv()
     lists_out[...] = lists_v[...]
-    for copy in copies:
+    turned[...] = jnp.zeros(turned.shape, turned.dtype)
+    for m in range(group):
+        for src in range(parts):
+            turned[m, src : src + 1, :] = lists_v[src, m : m + 1, :]
+    for copy in to_scalars(turned, scalars, lsem):
         copy.wait()
-    pick_rows(table, lists_s, group, members, some)
+    pick_rows(table, scalars, members, some)
     store = pltpu.make_async_copy(coeffs, coeffs_out, csem.at[0])
     shrink_groups(
         place, False, x.shape[1], some, sigma, members, coeffs, back, lists_v, same, energy, ebuf, egot, weights, esend, erecv, store.start
@@ -400,9 +397,7 @@
     def __init__(self, place, acc, own, got, sent, zgot, local, send, recv):
         self.place, self.acc, self.own, self.got, self.sent, self.zgot = place, acc, own, got, sent, zgot
         self.local, self.send, self.recv, self.started = local, send, recv, []
-        last = place.parts - 1
-        inner = jnp.where((place.part == 0) | (place.part == last), 0, 1)
-        self.order = [inner * (i + 1) + (1 - inner) * (last - i) for i in range(last)] + [0]
+        self.order = list(range(place.parts - 1, -1, -1))
 
     def start(self, copy):
         copy.start()
@@ -421,9 +416,9 @@
 
     def begin(self):
         place = self.place
-        for h in range(PIECES):
-            for d in sorted(range(1, place.ranks, 2), key=lambda d: lowest(d - 1, place.ranks)):
-                for off in self.order:
+        for d in sorted(range(1, place.ranks, 2), key=lambda d: lowest(d - 1, place.ranks)):
+            for off in self.order:
+                for h in range(PIECES):
                     self.start(
                         remote(
                             piece_of(self.acc.at[place.index(off, d)], h),
@@ -452,22 +447,21 @@
         place = self.place
         for level in place.bits[1:] + [place.ranks]:
             ds = [d for d in range(0, place.ranks, 2) if lowest(d, place.ranks) == level]
-            for h, d, i in itertools.product(range(PIECES), ds, range(place.parts)):
-                    off = self.order[i]
-                    piece = piece_of(self.sent.at[off, d // 2], h)
-                    piece[...] = self.value(off, d, h).astype(self.sent.dtype)
-                    if d == 0 and i == place.parts - 1:
-                        continue
-                    bit = lowest(d, 0)
-                    self.start(
-                        remote(
-                            piece,
-                            piece_of(self.got.at[off, d] if d else self.zgot.at[off], h),
-                            self.send.at[off, d, h],
-                            self.recv.at[off, d, h],
-                            place.device(0, bit) if d else place.device(off, 0),
-                        )
+            for d, off, h in itertools.product(ds, self.order, range(PIECES)):
+                piece = piece_of(self.sent.at[off, d // 2], h)
+                piece[...] = self.value(off, d, h).astype(self.sent.dtype)
+                if d == 0 and off == 0:
+                    continue
+                bit = lowest(d, 0)
+                self.start(
+                    remote(
+                        piece,
+                        piece_of(self.got.at[off, d] if d else self.zgot.at[off], h),
+                        self.send.at[off, d, h],
+                        self.recv.at[off, d, h],
+                        place.device(0, bit) if d else place.device(off, 0),
                     )
+                )
 
     def slices(self, h):
         place = self.place
@@ -534,16 +528,18 @@
     ]
 
 
-def second_kernel(count, some, acc, wsum, noisy, cube, cube_t, sigma, lists, lists_v, coeffs_in, basic, back, weights, *scratch):
+def second_kernel(count, some, acc, wsum, noisy, cube, cube_t, sigma, lists_v, turned, coeffs_in, basic, back, weights, *scratch):
     stage, got, table, send, recv = scratch[:5]
     members, same, energy, ebuf, egot, esend, erecv = scratch[5:12]
-    coeffs, csem = scratch[12:14]
+    coeffs, csem, lsem = scratch[12:15]
     group = members.shape[0]
+    scalars = scratch[15 : 15 + group]
     size = noisy.shape[0] // PIECES
     parts = stage.shape[0]
     place = Place(count, parts)
     fetch = pltpu.make_async_copy(coeffs_in, coeffs, csem.at[0])
     fetch.start()
+    copies = to_scalars(turned, scalars, lsem)
     spread = Spread(place, stage, got, table, send, recv)
     ebuf[...] = jnp.zeros(ebuf.shape, ebuf.dtype)
     collect = settle(
@@ -553,11 +549,13 @@
         noisy,
         cube,
         basic,
-        *scratch[14:],
+        *scratch[15 + group :],
         then=lambda h: spread.begin(h, basic[h * size : (h + 1) * size, :], cube_t),
     )
     spread.finish()
-    pick_rows(table, lists, group, members, some)
+    for copy in copies:
+        copy.wait()
+    pick_rows(table, scalars, members, some)
     fetch.wait()
     shrink_groups(
         place, True, noisy.shape[1], some, sigma, members, coeffs, back, lists_v, same, energy, ebuf, egot, weights, esend, erecv
@@ -570,11 +568,21 @@
     settle(Place(count, parts), acc, wsum, noisy, cube, out, *scratch).close()
 
 
-def add_kernel(count, some, lists, lists_v, weights, back, acc, wsum, members, *sums):
-    parts, group = lists.shape[0], members.shape[0]
-    each = LANES // group
+def add_kernel(count, some, carried, turned, weights, back, *refs):
+    group, refs_here = back.shape[:2]
+    parts = refs_here // some
+    kept = refs[:carried]
+    acc, wsum = refs[carried : carried + 2]
+    outs = refs[carried + 2 : 2 * carried + 2]
+    members, ksem, lsem = refs[2 * carried + 2 : 2 * carried + 5]
+    scalars = refs[2 * carried + 5 : 2 * carried + 5 + group]
+    sums = refs[2 * carried + 5 + group :]
     place = Place(count, parts)
     blocks, held = acc.shape[:2]
+    copies = to_scalars(turned, scalars, lsem)
+    moves = [pltpu.make_async_copy(src, dst, ksem.at[i]) for i, (src, dst) in enumerate(zip(kept, outs))]
+    for move in moves:
+        move.start()
 
     def clear(i, carry):
         rows = pl.ds(pl.multiple_of(i * LANES, LANES), LANES)
@@ -605,7 +613,7 @@
     def weigh(m, total):
         ones, loads = [], []
         for src in range(parts):
-            spots = lists_v[src, pl.ds(m, 1), :] - first
+            spots = turned[m, src : src + 1, :] - first
             loads.append(jnp.where((spots >> 7) == tall, heavy[src], 0.0).astype(jnp.bfloat16))
             ones.append(jnp.where((spots & (LANES - 1)) == low, 1.0, 0.0).astype(jnp.bfloat16))
         return total + lax.dot_general(
@@ -623,20 +631,22 @@
             wsum[b, per:, :] = jnp.zeros((SUBS - per, LANES), jnp.float32)
 
     together = group // STREAMS
+    for copy in copies:
+        copy.wait()
 
     def step(t, carry):
-        src, row = t // (some // each), lax.rem(t, some // each)
-        for q in range(each):
+        src, row = t // (some // SUBS), lax.rem(t, some // SUBS)
+        for q in range(SUBS):
             spots, news = [], []
             for m in range(group):
-                spot = lists[src, group + row, q * group + m]
+                spot = scalars[m][src, row * SUBS + q]
                 spots.append(spot)
-                news.append(sums[m // together][pl.ds(spot, 1), :] + members[m, pl.ds(t * each + q, 1), :])
+                news.append(sums[m // together][pl.ds(spot, 1), :] + members[m, pl.ds(t * SUBS + q, 1), :])
             for m in range(group):
                 sums[m // together][pl.ds(spots[m], 1), :] = news[m]
         return carry
 
-    lax.fori_loop(0, parts * some // each, step, 0)
+    lax.fori_loop(0, refs_here // SUBS, step, 0)
 
     def store(b, carry):
         for i in range(held // LANES):
@@ -648,6 +658,8 @@
         return carry
 
     lax.fori_loop(0, blocks, store, 0)
+    for move in moves:
+        move.wait()
 
 
 def shape(*dims, dtype=jnp.float32):
@@ -661,19 +673,21 @@
     )
 
 
-def add_up(count, some, held, lists, weights, back):
-    parts, group = lists.shape[0], back.shape[0]
-    ranks = count // parts
+def add_up(count, some, held, turned, weights, back, *kept):
+    group, refs = back.shape[:2]
+    ranks = count // (refs // some)
     return pl.pallas_call(
-        functools.partial(add_kernel, count, some),
-        out_shape=[shape(count, held, LANES, dtype=back.dtype), shape(ranks, SUBS, LANES)],
-        in_specs=[SMEM, VMEM, VMEM, VMEM],
-        out_specs=[VMEM, VMEM],
-        scratch_shapes=[pltpu.VMEM((group, parts * some, LANES), jnp.float32)]
+        functools.partial(add_kernel, count, some, len(kept)),
+        out_shape=[shape(count, held, LANES, dtype=back.dtype), shape(ranks, SUBS, LANES)]
+        + [shape(*each.shape, dtype=each.dtype) for each in kept],
+        in_specs=[VMEM, VMEM, VMEM] + [VMEM] * len(kept),
+        out_specs=[VMEM, VMEM] + [HBM] * len(kept),
+        scratch_shapes=[pltpu.VMEM((group, refs, LANES), jnp.float32), SEMS((1,)), SEMS((group,))]
+        + [pltpu.SMEM((SUBS, LANES), jnp.int32)] * group
         + [pltpu.VMEM((count * held, LANES), jnp.float32)] * STREAMS,
         compiler_params=params(count * held),
         name="add_up",
-    )(lists, lists, weights, back)
+    )(turned, weights, back, *kept)
 
 
 def body(noisy, matches, cube_home, sigma_coef):
@@ -686,16 +700,17 @@
     sigma = sigma_coef[None, :]
     dtype = noisy.dtype
     shared = spread_scratch(count, parts, held, dtype) + shrink_scratch(parts, group, refs)
-    coeffs, back, weights, lists = pl.pallas_call(
+    coeffs, back, weights, lists, turned = pl.pallas_call(
         functools.partial(first_kernel, count),
         out_shape=[
             shape(group, refs, LANES),
             shape(group, refs, LANES, dtype=dtype),
             shape(SUBS, LANES),
-            shape(parts, 2 * group, LANES, dtype=jnp.int32),
+            shape(parts, group, LANES, dtype=jnp.int32),
+            shape(group, SUBS, LANES, dtype=jnp.int32),
         ],
         in_specs=[HBM] * 5,
-        out_specs=[HBM] + [VMEM] * 3,
+        out_specs=[HBM] + [VMEM] * 4,
         scratch_shapes=shared
         + [
             pltpu.VMEM(noisy.shape, dtype),
@@ -706,17 +721,17 @@
             pltpu.VMEM((group, refs, LANES), jnp.float32),
             SEMS((1,)),
             pltpu.SMEM(cube_home.shape, jnp.int32),
-            pltpu.SMEM((2 * group, LANES), jnp.int32),
-            pltpu.VMEM((parts, 2 * group, LANES), jnp.int32),
-            pltpu.SMEM((parts, 2 * group, LANES), jnp.int32),
+            pltpu.SMEM((group, LANES), jnp.int32),
+            pltpu.VMEM((parts, group, LANES), jnp.int32),
             SEMS((parts,)),
             SEMS((parts,)),
-            SEMS((parts,)),
-        ],
+            SEMS((group,)),
+        ]
+        + [pltpu.SMEM((SUBS, LANES), jnp.int32)] * group,
         compiler_params=params(count * held, 0),
         name="shrink",
     )(*[pltpu.with_memory_space_constraint(v, pltpu.HBM) for v in (noisy, cube_home, matches.T, sigma, jnp.asarray(cube_t))])
-    acc, wsum = add_up(count, some, held, lists, weights, back)
+    acc, wsum = add_up(count, some, held, turned, weights, back)
     basic, back, weights = pl.pallas_call(
         functools.partial(second_kernel, count, some),
         out_shape=[
@@ -724,15 +739,16 @@
             shape(group, refs, LANES, dtype=dtype),
             shape(SUBS, LANES),
         ],
-        in_specs=[HBM] + [VMEM] * 5 + [SMEM, VMEM, HBM],
+        in_specs=[HBM] + [VMEM] * 7 + [HBM],
         out_specs=[VMEM] * 3,
         scratch_shapes=shared
-        + [pltpu.VMEM((group, refs, LANES), jnp.float32), SEMS((1,))]
+        + [pltpu.VMEM((group, refs, LANES), jnp.float32), SEMS((1,)), SEMS((group,))]
+        + [pltpu.SMEM((SUBS, LANES), jnp.int32)] * group
         + settle_scratch(count, parts, held, dtype),
         compiler_params=params(count * held, 1),
         name="wiener",
-    )(acc, wsum, noisy, cube, cube_t, sigma, lists, lists, coeffs)
-    acc, wsum = add_up(count, some, held, lists, weights, back)
+    )(acc, wsum, noisy, cube, cube_t, sigma, lists, turned, coeffs)
+    acc, wsum, basic = add_up(count, some, held, turned, weights, back, basic)
     final = pl.pallas_call(
         functools.partial(third_kernel, count, parts),
         out_shape=shape(held, width, dtype=dtype),

time: 135 us -> 126 us (0.933)
  Pallas kernels: 133 us -> 124 us
    pallas_call x2, Pallas kernels: 21.4 us -> 17.4 us  [add_up(): pl.pallas_call(functools.partial(add_kernel, count, some, len(kept)), out...]
    pallas_call x1, Pallas kernels: 51.7 us -> 49 us  [body(): pl.pallas_call(functools.partial(second_kernel, count, some), out_shape=[...]
where the time goes in v4:
time: 126 us
  Pallas kernels  124 us (98%)
    pallas_call x1, Pallas kernels, body(): pl.pallas_call(functools.partial(second_kernel, count, some), out_shape=[...  49 us
    pallas_call x1, Pallas kernels, body(): pl.pallas_call(functools.partial(first_kernel, count), out_shape=[shape(g...  37 us
    pallas_call x1, Pallas kernels, body(): pl.pallas_call(functools.partial(third_kernel, count, parts), out_shape=s...  21.1 us
    pallas_call x2, Pallas kernels, add_up(): pl.pallas_call(functools.partial(add_kernel, count, some, len(kept)), out...  17.4 us

profile of v4, /device:TPU:0, one launch (start us, length us, event | category | flops | bytes accessed | tf_op | source)
XLA Modules:
  0.0 126.0 jit_solution(10917858763491927258)
XLA Ops:
  0.6 0.0 copy-start.2
  0.6 0.0 copy-start.1
  0.7 0.0 copy-start
  0.7 0.0 copy-start.3
  0.7 37.0 %shrink.1 = (f32[16,384,128]{2,1,0:T(8,128)S(1)}, bf16[16,384,128]{2,1,0:T(8,128)(2,1)S(1)}, f32[8,128]{1,0:T(8,128)S(1)}, s32[4,16,128]{2,1,0:T(8,128)S(1)}, s32[16,8,128]{2,1,0:T(8,128)S(1)}) custom-call(bf16[512,512]{1,0:T(8,128)(2,1)} %noisy.3, s32[8192]{0:T(1024)} %home_in.1, s32[16,96]{1,0:T(8,128)} %bitcast.4, f32[1,512]{1,0:T(1,128)} %bitcast.2, ...), custom_call_target="tpu_custom_call" | custom-call | tf_op jit(solution)/shard_map/shrink/pallas_call | solution.py:703
  37.7 8.7 %add_up.2 = (bf16[16,512,128]{2,1,0:T(8,128)(2,1)S(1)}, f32[4,8,128]{2,1,0:T(8,128)S(1)}) custom-call(s32[16,8,128]{2,1,0:T(8,128)S(1)} %get-tuple-element.15.turned, f32[8,128]{1,0:T(8,128)S(1)} %get-tuple-element.16.weights, bf16[16,384,128]{2,1,0:T(8,128)(2,1)S(1)} %get-tuple-element.17.back), custom_call_target="tpu_custom_call" | custom-call | tf_op jit(solution)/shard_map/add_up/pallas_call | solution.py:679
  46.3 0.0 copy-done.2
  46.3 0.0 copy-done.1
  46.4 0.0 copy-done
  46.4 0.0 copy-done.3
  46.4 49.0 %wiener.1 = (bf16[512,512]{1,0:T(8,128)(2,1)S(1)}, bf16[16,384,128]{2,1,0:T(8,128)(2,1)S(1)}, f32[8,128]{1,0:T(8,128)S(1)}) custom-call(bf16[16,512,128]{2,1,0:T(8,128)(2,1)S(1)} %get-tuple-element.18.acc, f32[4,8,128]{2,1,0:T(8,128)S(1)} %get-tuple-element.19.wsum, bf16[512,512]{1,0:T(8,128)(2,1)S(1)} %copy-done, bf16[512,512]{1,0:T(8,128)(2,1)S(1)} %copy-done.1, ...), custom_call_target="tpu_custom_call" | custom-call | tf_op jit(solution)/shard_map/wiener/pallas_call | solution.py:735
  95.4 8.7 %add_up.3 = (bf16[16,512,128]{2,1,0:T(8,128)(2,1)S(1)}, f32[4,8,128]{2,1,0:T(8,128)S(1)}, bf16[512,512]{1,0:T(8,128)(2,1)}) custom-call(s32[16,8,128]{2,1,0:T(8,128)S(1)} %get-tuple-element.15.turned, f32[8,128]{1,0:T(8,128)S(1)} %get-tuple-element.22.weights, bf16[16,384,128]{2,1,0:T(8,128)(2,1)S(1)} %get-tuple-element.23.back, ...), custom_call_target="tpu_custom_call" | custom-call | tf_op jit(solution)/shard_map/add_up/pallas_call | solution.py:679
  104.1 21.1 %settle.1 = bf16[512,512]{1,0:T(8,128)(2,1)S(1)} custom-call(bf16[16,512,128]{2,1,0:T(8,128)(2,1)S(1)} %get-tuple-element.26.acc, f32[4,8,128]{2,1,0:T(8,128)S(1)} %get-tuple-element.27.wsum, bf16[512,512]{1,0:T(8,128)(2,1)S(1)} %copy-done, bf16[512,512]{1,0:T(8,128)(2,1)S(1)} %copy-done.1), custom_call_target="tpu_custom_call" | custom-call | tf_op jit(solution)/shard_map/settle/pallas_call | solution.py:752
  125.2 0.8 copy.9
Async XLA Ops:
  0.6 45.7 %copy-start.2 = (bf16[512,512]{1,0:T(8,128)(2,1)S(1)}, bf16[512,512]{1,0:T(8,128)(2,1)}, u32[]{:S(2)}) copy-start(bf16[512,512]{1,0:T(8,128)(2,1)} %constant.4.clone.cube_in.cube_t) | copy-start | bytes 1572868
  0.6 45.7 %copy-start.1 = (bf16[512,512]{1,0:T(8,128)(2,1)S(1)}, bf16[512,512]{1,0:T(8,128)(2,1)}, u32[]{:S(2)}) copy-start(bf16[512,512]{1,0:T(8,128)(2,1)} %constant.5.clone.cube) | copy-start | bytes 1572868
  0.7 45.7 %copy-start = (bf16[512,512]{1,0:T(8,128)(2,1)S(1)}, bf16[512,512]{1,0:T(8,128)(2,1)}, u32[]{:S(2)}) copy-start(bf16[512,512]{1,0:T(8,128)(2,1)} %noisy.3) | copy-start | bytes 1572868
  0.7 45.7 %copy-start.3 = (f32[512]{0:T(512)S(1)}, f32[512]{0:T(512)}, u32[]{:S(2)}) copy-start(f32[512]{0:T(512)} %param.9) | copy-start | bytes 6148

commit v5 on v4

--- a/solution.py
+++ b/solution.py
@@ -142,11 +142,13 @@
                 copy.start()
                 self.started.append(copy)
 
-    def begin(self, h, rows, cube_t):
+    def begin(self, hs, rows, cube_t):
         place = self.place
-        for off in list(range(1, place.parts)) + [0]:
+        size = rows.shape[0] // PIECES
+        for off, h in itertools.product(list(range(1, place.parts)) + [0], hs):
             columns = pl.ds(pl.multiple_of(flip(place.part, off) * LANES, LANES), LANES)
-            spec = jnp.dot(rows, cube_t[:, columns], preferred_element_type=jnp.float32)
+            part = rows[h * size : (h + 1) * size, :]
+            spec = jnp.dot(part, cube_t[:, columns], preferred_element_type=jnp.float32)
             piece = piece_of(self.stage.at[off], h)
             piece[...] = spec.astype(self.stage.dtype)
             if off == 0:
@@ -170,7 +172,7 @@
         rows = pl.ds(pl.multiple_of(first, size), size)
         self.table[rows, :] = source[...].astype(jnp.float32)
 
-    def finish(self):
+    def finish(self, then=None):
         place = self.place
 
         def when(key):
@@ -193,6 +195,8 @@
             ).wait_recv()
             self.pass_on(off, d, h)
             self.widen(off, d, h)
+            if then is not None and (off, d, h) == (place.parts - 1, 0, PIECES - 1):
+                then()
 
     def close(self):
         for copy in self.started:
@@ -244,7 +248,7 @@
     return lax.broadcasted_iota(jnp.int32, shape, 0) == lax.broadcasted_iota(jnp.int32, shape, 1)
 
 
-def shrink_groups(place, second, width, some, sigma, members, coeffs, back, lists_v, same, energy, ebuf, egot, weights, send, recv, then=None):
+def shrink_groups(place, second, width, some, sigma, members, coeffs, back, same, energy, ebuf, egot, weights, send, recv, then=None):
     group, refs = members.shape[:2]
     factor = scales(group)
     columns = pl.ds(pl.multiple_of(place.part * LANES, LANES), LANES)
@@ -282,8 +286,6 @@
         copy.start()
         started.append(copy)
 
-    find_equals(lists_v, same, group, some)
-
     def inverse(b, carry):
         rows = pl.ds(pl.multiple_of(b * 2 * SUBS, 2 * SUBS), 2 * SUBS)
         values = cosine_sums_transposed([members[j, rows, :] * factor[j] for j in range(group)])
@@ -310,7 +312,6 @@
     return [
         pltpu.VMEM((group, refs, LANES), jnp.float32),
         pltpu.VMEM((refs, LANES), jnp.float32),
-        pltpu.VMEM((refs, LANES), jnp.float32),
         pltpu.VMEM((SUBS, LANES), jnp.float32),
         pltpu.VMEM((parts, SUBS, LANES), jnp.float32),
         SEMS((parts,)),
@@ -318,15 +319,14 @@
     ]
 
 
-def first_kernel(count, x_in, home_in, ids_in, sigma_in, cube_in, coeffs_out, back, weights, lists_out, turned, *scratch):
+def first_kernel(count, x_in, home_in, ids_in, sigma_in, cube_in, coeffs_out, back, weights, same, turned, *scratch):
     stage, got, table, send, recv = scratch[:5]
-    members, same, energy, ebuf, egot, esend, erecv = scratch[5:12]
-    x, cube_t, sigma, ids, insem = scratch[12:17]
-    coeffs, csem, home, named, lists_v, lsend, lrecv, lsem = scratch[17:25]
-    scalars = scratch[25:]
+    members, energy, ebuf, egot, esend, erecv = scratch[5:11]
+    x, cube_t, sigma, ids, insem = scratch[11:16]
+    coeffs, csem, home, named, lists_v, lsend, lrecv, lsem = scratch[16:24]
+    scalars = scratch[24:]
     parts = stage.shape[0]
     group, some = ids.shape
-    size = x.shape[0] // PIECES
     place = Place(count, parts)
     pairs = [(x_in, x), (cube_in, cube_t), (home_in, home), (ids_in, ids), (sigma_in, sigma)]
     fetches = [pltpu.make_async_copy(src, dst, insem.at[i]) for i, (src, dst) in enumerate(pairs)]
@@ -336,8 +336,7 @@
     for fetch in fetches[:2]:
         fetch.wait()
     spread = Spread(place, stage, got, table, send, recv)
-    for h in range(PIECES):
-        spread.begin(h, x[h * size : (h + 1) * size, :], cube_t)
+    spread.begin(range(PIECES), x, cube_t)
 
     def look_up(row, carry):
         for q in range(SUBS):
@@ -371,21 +370,26 @@
         )
         copy.start()
         started.append(copy)
-    spread.finish()
-    for off in range(1, parts):
-        source = lists_v.at[flip(place.part, off)]
-        remote(source, source, lsend.at[off], lrecv.at[off], place.device(off, 0)).wait_recv()
-    lists_out[...] = lists_v[...]
-    turned[...] = jnp.zeros(turned.shape, turned.dtype)
-    for m in range(group):
-        for src in range(parts):
-            turned[m, src : src + 1, :] = lists_v[src, m : m + 1, :]
-    for copy in to_scalars(turned, scalars, lsem):
+    copies = []
+
+    def lists_ready():
+        for off in range(1, parts):
+            source = lists_v.at[flip(place.part, off)]
+            remote(source, source, lsend.at[off], lrecv.at[off], place.device(off, 0)).wait_recv()
+        turned[...] = jnp.zeros(turned.shape, turned.dtype)
+        for m in range(group):
+            for src in range(parts):
+                turned[m, src : src + 1, :] = lists_v[src, m : m + 1, :]
+        find_equals(lists_v, same, group, some)
+        copies.extend(to_scalars(turned, scalars, lsem))
+
+    spread.finish(lists_ready)
+    for copy in copies:
         copy.wait()
     pick_rows(table, scalars, members, some)
     store = pltpu.make_async_copy(coeffs, coeffs_out, csem.at[0])
     shrink_groups(
-        place, False, x.shape[1], some, sigma, members, coeffs, back, lists_v, same, energy, ebuf, egot, weights, esend, erecv, store.start
+        place, False, x.shape[1], some, sigma, members, coeffs, back, same, energy, ebuf, egot, weights, esend, erecv, store.start
     )
     store.wait()
     for copy in started:
@@ -394,25 +398,14 @@
 
 
 class Collect:
-    def __init__(self, place, acc, own, got, sent, zgot, local, send, recv):
-        self.place, self.acc, self.own, self.got, self.sent, self.zgot = place, acc, own, got, sent, zgot
-        self.local, self.send, self.recv, self.started = local, send, recv, []
+    def __init__(self, place, acc, got, sent, zgot, send, recv):
+        self.place, self.acc, self.got, self.sent, self.zgot = place, acc, got, sent, zgot
+        self.send, self.recv, self.started = send, recv, []
         self.order = list(range(place.parts - 1, -1, -1))
 
     def start(self, copy):
         copy.start()
         self.started.append(copy)
-
-    def fetch(self, off, d):
-        return pltpu.make_async_copy(
-            self.acc.at[self.place.index(off, d)], self.own.at[off, d // 2], self.local.at[off, d // 2]
-        )
-
-    def open(self):
-        place = self.place
-        for d in sorted(range(0, place.ranks, 2), key=lambda d: lowest(d, place.ranks)):
-            for off in self.order:
-                self.fetch(off, d).start()
 
     def begin(self):
         place = self.place
@@ -431,9 +424,7 @@
 
     def value(self, off, d, h):
         place = self.place
-        if h == 0:
-            self.fetch(off, d).wait()
-        total = piece_of(self.own.at[off, d // 2], h)[...].astype(jnp.float32)
+        total = piece_of(self.acc.at[place.index(off, d)], h)[...].astype(jnp.float32)
         for bit in place.bits:
             if bit < lowest(d, place.ranks):
                 piece = piece_of(self.got.at[off, d | bit], h)
@@ -444,24 +435,26 @@
         return total
 
     def run(self):
+        for level in self.place.bits[1:] + [self.place.ranks]:
+            self.hand_on([d for d in range(0, self.place.ranks, 2) if lowest(d, self.place.ranks) == level])
+
+    def hand_on(self, ds):
         place = self.place
-        for level in place.bits[1:] + [place.ranks]:
-            ds = [d for d in range(0, place.ranks, 2) if lowest(d, place.ranks) == level]
-            for d, off, h in itertools.product(ds, self.order, range(PIECES)):
-                piece = piece_of(self.sent.at[off, d // 2], h)
-                piece[...] = self.value(off, d, h).astype(self.sent.dtype)
-                if d == 0 and off == 0:
-                    continue
-                bit = lowest(d, 0)
-                self.start(
-                    remote(
-                        piece,
-                        piece_of(self.got.at[off, d] if d else self.zgot.at[off], h),
-                        self.send.at[off, d, h],
-                        self.recv.at[off, d, h],
-                        place.device(0, bit) if d else place.device(off, 0),
-                    )
+        for d, off, h in itertools.product(ds, self.order, range(PIECES)):
+            piece = piece_of(self.sent.at[off, d // 2], h)
+            piece[...] = self.value(off, d, h).astype(self.sent.dtype)
+            if d == 0 and off == 0:
+                continue
+            bit = lowest(d, 0)
+            self.start(
+                remote(
+                    piece,
+                    piece_of(self.got.at[off, d] if d else self.zgot.at[off], h),
+                    self.send.at[off, d, h],
+                    self.recv.at[off, d, h],
+                    place.device(0, bit) if d else place.device(off, 0),
                 )
+            )
 
     def slices(self, h):
         place = self.place
@@ -478,10 +471,9 @@
             copy.wait_send()
 
 
-def settle(place, acc, wsum, noisy, cube, out, own, got, sent, zgot, wgot, local, send, recv, wsend, wrecv, then=None):
+def settle(place, acc, wsum, noisy, cube, out, got, sent, zgot, wgot, send, recv, wsend, wrecv, then=None):
     held = noisy.shape[0]
-    collect = Collect(place, acc, own, got, sent, zgot, local, send, recv)
-    collect.open()
+    collect = Collect(place, acc, got, sent, zgot, send, recv)
     place.greet()
     collect.begin()
     for d in range(1, place.ranks):
@@ -515,12 +507,10 @@
     ranks = count // parts
     half = (parts, ranks // 2, held, LANES)
     return [
-        pltpu.VMEM(half, dtype),
         pltpu.VMEM((parts, ranks, held, LANES), dtype),
         pltpu.VMEM(half, dtype),
         pltpu.VMEM((parts, held, LANES), dtype),
         pltpu.VMEM((ranks, SUBS, LANES), jnp.float32),
-        SEMS((parts, ranks // 2)),
         SEMS((parts, ranks, PIECES)),
         SEMS((parts, ranks, PIECES)),
         SEMS((ranks,)),
@@ -528,13 +518,12 @@
     ]
 
 
-def second_kernel(count, some, acc, wsum, noisy, cube, cube_t, sigma, lists_v, turned, coeffs_in, basic, back, weights, *scratch):
+def second_kernel(count, some, acc, wsum, noisy, cube, cube_t, sigma, turned, same, coeffs_in, basic, back, weights, *scratch):
     stage, got, table, send, recv = scratch[:5]
-    members, same, energy, ebuf, egot, esend, erecv = scratch[5:12]
-    coeffs, csem, lsem = scratch[12:15]
+    members, energy, ebuf, egot, esend, erecv = scratch[5:11]
+    coeffs, csem, lsem = scratch[11:14]
     group = members.shape[0]
-    scalars = scratch[15 : 15 + group]
-    size = noisy.shape[0] // PIECES
+    scalars = scratch[14 : 14 + group]
     parts = stage.shape[0]
     place = Place(count, parts)
     fetch = pltpu.make_async_copy(coeffs_in, coeffs, csem.at[0])
@@ -549,8 +538,8 @@
         noisy,
         cube,
         basic,
-        *scratch[15 + group :],
-        then=lambda h: spread.begin(h, basic[h * size : (h + 1) * size, :], cube_t),
+        *scratch[14 + group :],
+        then=lambda h: spread.begin([h], basic, cube_t),
     )
     spread.finish()
     for copy in copies:
@@ -558,7 +547,7 @@
     pick_rows(table, scalars, members, some)
     fetch.wait()
     shrink_groups(
-        place, True, noisy.shape[1], some, sigma, members, coeffs, back, lists_v, same, energy, ebuf, egot, weights, esend, erecv
+        place, True, noisy.shape[1], some, sigma, members, coeffs, back, same, energy, ebuf, egot, weights, esend, erecv
     )
     collect.close()
     spread.close()
@@ -680,7 +669,7 @@
         functools.partial(add_kernel, count, some, len(kept)),
         out_shape=[shape(count, held, LANES, dtype=back.dtype), shape(ranks, SUBS, LANES)]
         + [shape(*each.shape, dtype=each.dtype) for each in kept],
-        in_specs=[VMEM, VMEM, VMEM] + [VMEM] * len(kept),
+        in_specs=[VMEM] * (3 + len(kept)),
         out_specs=[VMEM, VMEM] + [HBM] * len(kept),
         scratch_shapes=[pltpu.VMEM((group, refs, LANES), jnp.float32), SEMS((1,)), SEMS((group,))]
         + [pltpu.SMEM((SUBS, LANES), jnp.int32)] * group
@@ -700,13 +689,13 @@
     sigma = sigma_coef[None, :]
     dtype = noisy.dtype
     shared = spread_scratch(count, parts, held, dtype) + shrink_scratch(parts, group, refs)
-    coeffs, back, weights, lists, turned = pl.pallas_call(
+    coeffs, back, weights, same, turned = pl.pallas_call(
         functools.partial(first_kernel, count),
         out_shape=[
             shape(group, refs, LANES),
             shape(group, refs, LANES, dtype=dtype),
             shape(SUBS, LANES),
-            shape(parts, group, LANES, dtype=jnp.int32),
+            shape(refs, LANES),
             shape(group, SUBS, LANES, dtype=jnp.int32),
         ],
         in_specs=[HBM] * 5,
@@ -739,7 +728,7 @@
             shape(group, refs, LANES, dtype=dtype),
             shape(SUBS, LANES),
         ],
-        in_specs=[HBM] + [VMEM] * 7 + [HBM],
+        in_specs=[VMEM] * 8 + [HBM],
         out_specs=[VMEM] * 3,
         scratch_shapes=shared
         + [pltpu.VMEM((group, refs, LANES), jnp.float32), SEMS((1,)), SEMS((group,))]
@@ -747,12 +736,12 @@
         + settle_scratch(count, parts, held, dtype),
         compiler_params=params(count * held, 1),
         name="wiener",
-    )(acc, wsum, noisy, cube, cube_t, sigma, lists, turned, coeffs)
+    )(acc, wsum, noisy, cube, cube_t, sigma, turned, same, coeffs)
     acc, wsum, basic = add_up(count, some, held, turned, weights, back, basic)
     final = pl.pallas_call(
         functools.partial(third_kernel, count, parts),
         out_shape=shape(held, width, dtype=dtype),
-        in_specs=[HBM] + [VMEM] * 3,
+        in_specs=[VMEM] * 4,
         out_specs=VMEM,
         scratch_shapes=settle_scratch(count, parts, held, dtype),
         compiler_params=params(count * held, 2),

time: 126 us -> 122 us (0.968)
  Pallas kernels: 124 us -> 120 us
    pallas_call x1, Pallas kernels: 37 us -> 34.6 us  [body(): pl.pallas_call(functools.partial(first_kernel, count), out_shape=[shape(g...]
where the time goes in v5:
time: 122 us
  Pallas kernels  120 us (98%)
    pallas_call x1, Pallas kernels, body(): pl.pallas_call(functools.partial(second_kernel, count, some), out_shape=[...  47.8 us
    pallas_call x1, Pallas kernels, body(): pl.pallas_call(functools.partial(first_kernel, count), out_shape=[shape(g...  34.6 us
    pallas_call x1, Pallas kernels, body(): pl.pallas_call(functools.partial(third_kernel, count, parts), out_shape=s...  20.6 us
    pallas_call x2, Pallas kernels, add_up(): pl.pallas_call(functools.partial(add_kernel, count, some, len(kept)), out...  17.4 us

profile of v5, /device:TPU:0, one launch (start us, length us, event | category | flops | bytes accessed | tf_op | source)
XLA Modules:
  0.0 121.9 jit_solution(12265638914737666951)
XLA Ops:
  0.6 0.0 copy-start.2
  0.6 0.0 copy-start.1
  0.7 0.0 copy-start
  0.7 0.0 copy-start.3
  0.7 34.6 %shrink.1 = (f32[16,384,128]{2,1,0:T(8,128)S(1)}, bf16[16,384,128]{2,1,0:T(8,128)(2,1)S(1)}, f32[8,128]{1,0:T(8,128)S(1)}, f32[384,128]{1,0:T(8,128)S(1)}, s32[16,8,128]{2,1,0:T(8,128)S(1)}) custom-call(bf16[512,512]{1,0:T(8,128)(2,1)} %noisy.3, s32[8192]{0:T(1024)} %home_in.1, s32[16,96]{1,0:T(8,128)} %bitcast.4, f32[1,512]{1,0:T(1,128)} %bitcast.2, ...), custom_call_target="tpu_custom_call" | custom-call | tf_op jit(solution)/shard_map/shrink/pallas_call | solution.py:692
  35.3 8.7 %add_up.2 = (bf16[16,512,128]{2,1,0:T(8,128)(2,1)S(1)}, f32[4,8,128]{2,1,0:T(8,128)S(1)}) custom-call(s32[16,8,128]{2,1,0:T(8,128)S(1)} %get-tuple-element.15.turned, f32[8,128]{1,0:T(8,128)S(1)} %get-tuple-element.16.weights, bf16[16,384,128]{2,1,0:T(8,128)(2,1)S(1)} %get-tuple-element.17.back), custom_call_target="tpu_custom_call" | custom-call | tf_op jit(solution)/shard_map/add_up/pallas_call | solution.py:668
  43.9 0.0 copy-done.2
  43.9 0.0 copy-done.1
  44.0 0.0 copy-done
  44.0 0.0 copy-done.3
  44.0 47.8 %wiener.1 = (bf16[512,512]{1,0:T(8,128)(2,1)S(1)}, bf16[16,384,128]{2,1,0:T(8,128)(2,1)S(1)}, f32[8,128]{1,0:T(8,128)S(1)}) custom-call(bf16[16,512,128]{2,1,0:T(8,128)(2,1)S(1)} %get-tuple-element.18.acc, f32[4,8,128]{2,1,0:T(8,128)S(1)} %get-tuple-element.19.wsum, bf16[512,512]{1,0:T(8,128)(2,1)S(1)} %copy-done, bf16[512,512]{1,0:T(8,128)(2,1)S(1)} %copy-done.1, ...), custom_call_target="tpu_custom_call" | custom-call | tf_op jit(solution)/shard_map/wiener/pallas_call | solution.py:724
  91.7 8.7 %add_up.3 = (bf16[16,512,128]{2,1,0:T(8,128)(2,1)S(1)}, f32[4,8,128]{2,1,0:T(8,128)S(1)}, bf16[512,512]{1,0:T(8,128)(2,1)}) custom-call(s32[16,8,128]{2,1,0:T(8,128)S(1)} %get-tuple-element.15.turned, f32[8,128]{1,0:T(8,128)S(1)} %get-tuple-element.22.weights, bf16[16,384,128]{2,1,0:T(8,128)(2,1)S(1)} %get-tuple-element.23.back, ...), custom_call_target="tpu_custom_call" | custom-call | tf_op jit(solution)/shard_map/add_up/pallas_call | solution.py:668
  100.4 20.6 %settle.1 = bf16[512,512]{1,0:T(8,128)(2,1)S(1)} custom-call(bf16[16,512,128]{2,1,0:T(8,128)(2,1)S(1)} %get-tuple-element.26.acc, f32[4,8,128]{2,1,0:T(8,128)S(1)} %get-tuple-element.27.wsum, bf16[512,512]{1,0:T(8,128)(2,1)S(1)} %copy-done, bf16[512,512]{1,0:T(8,128)(2,1)S(1)} %copy-done.1), custom_call_target="tpu_custom_call" | custom-call | tf_op jit(solution)/shard_map/settle/pallas_call | solution.py:741
  121.1 0.8 copy.9
Async XLA Ops:
  0.6 43.3 %copy-start.2 = (bf16[512,512]{1,0:T(8,128)(2,1)S(1)}, bf16[512,512]{1,0:T(8,128)(2,1)}, u32[]{:S(2)}) copy-start(bf16[512,512]{1,0:T(8,128)(2,1)} %constant.4.clone.cube_in.cube_t) | copy-start | bytes 1572868
  0.6 43.3 %copy-start.1 = (bf16[512,512]{1,0:T(8,128)(2,1)S(1)}, bf16[512,512]{1,0:T(8,128)(2,1)}, u32[]{:S(2)}) copy-start(bf16[512,512]{1,0:T(8,128)(2,1)} %constant.5.clone.cube) | copy-start | bytes 1572868
  0.7 43.3 %copy-start = (bf16[512,512]{1,0:T(8,128)(2,1)S(1)}, bf16[512,512]{1,0:T(8,128)(2,1)}, u32[]{:S(2)}) copy-start(bf16[512,512]{1,0:T(8,128)(2,1)} %noisy.3) | copy-start | bytes 1572868
  0.7 43.3 %copy-start.3 = (f32[512]{0:T(512)S(1)}, f32[512]{0:T(512)}, u32[]{:S(2)}) copy-start(f32[512]{0:T(512)} %param.9) | copy-start | bytes 6148

commit v6 on v5

--- a/solution.py
+++ b/solution.py
@@ -101,12 +101,16 @@
     def device(self, off, d):
         return {"space": self.index(off, d)}
 
+    def peers(self):
+        return [(off, 0) for off in range(1, self.parts)] + [(0, d) for d in range(1, self.ranks)]
+
     def greet(self):
         barrier = pltpu.get_barrier_semaphore()
-        peers = [(off, 0) for off in range(1, self.parts)] + [(0, d) for d in range(1, self.ranks)]
-        for off, d in peers:
+        for off, d in self.peers():
             pl.semaphore_signal(barrier, inc=1, device_id=self.device(off, d), device_id_type=MESH)
-        pl.semaphore_wait(barrier, len(peers))
+
+    def meet(self):
+        pl.semaphore_wait(pltpu.get_barrier_semaphore(), len(self.peers()))
 
 
 def remote(src, dst, send, recv, device):
@@ -142,24 +146,28 @@
                 copy.start()
                 self.started.append(copy)
 
-    def begin(self, hs, rows, cube_t):
-        place = self.place
+    def orders(self, hs):
+        return itertools.product(list(range(1, self.place.parts)) + [0], hs)
+
+    def transform(self, hs, rows, cube_t):
         size = rows.shape[0] // PIECES
-        for off, h in itertools.product(list(range(1, place.parts)) + [0], hs):
-            columns = pl.ds(pl.multiple_of(flip(place.part, off) * LANES, LANES), LANES)
+        for off, h in self.orders(hs):
+            columns = pl.ds(pl.multiple_of(flip(self.place.part, off) * LANES, LANES), LANES)
             part = rows[h * size : (h + 1) * size, :]
             spec = jnp.dot(part, cube_t[:, columns], preferred_element_type=jnp.float32)
-            piece = piece_of(self.stage.at[off], h)
-            piece[...] = spec.astype(self.stage.dtype)
+            piece_of(self.stage.at[off], h)[...] = spec.astype(self.stage.dtype)
+
+    def begin(self, hs):
+        for off, h in self.orders(hs):
             if off == 0:
                 self.pass_on(0, 0, h)
                 continue
             copy = remote(
-                piece,
+                piece_of(self.stage.at[off], h),
                 piece_of(self.got.at[off, 0], h),
                 self.send.at[off, 0, h],
                 self.recv.at[off, 0, h],
-                place.device(off, 0),
+                self.place.device(off, 0),
             )
             copy.start()
             self.started.append(copy)
@@ -287,7 +295,7 @@
         started.append(copy)
 
     def inverse(b, carry):
-        rows = pl.ds(pl.multiple_of(b * 2 * SUBS, 2 * SUBS), 2 * SUBS)
+        rows = pl.ds(pl.multiple_of(b * SUBS, SUBS), SUBS)
         values = cosine_sums_transposed([members[j, rows, :] * factor[j] for j in range(group)])
         for m in range(group):
             merged = values[m]
@@ -297,7 +305,7 @@
             back[m, rows, :] = merged.astype(back.dtype)
         return carry
 
-    lax.fori_loop(0, refs // (2 * SUBS), inverse, 0)
+    lax.fori_loop(0, refs // SUBS, inverse, 0)
     total = ebuf[...]
     for off in range(1, place.parts):
         remote(ebuf, egot.at[off], send.at[off], recv.at[off], place.device(off, 0)).wait_recv()
@@ -336,7 +344,9 @@
     for fetch in fetches[:2]:
         fetch.wait()
     spread = Spread(place, stage, got, table, send, recv)
-    spread.begin(range(PIECES), x, cube_t)
+    spread.transform(range(PIECES), x, cube_t)
+    place.meet()
+    spread.begin(range(PIECES))
 
     def look_up(row, carry):
         for q in range(SUBS):
@@ -471,10 +481,43 @@
             copy.wait_send()
 
 
-def settle(place, acc, wsum, noisy, cube, out, got, sent, zgot, wgot, send, recv, wsend, wrecv, then=None):
+def weigh_rows(place, some, held, turned, weights, wsum):
+    parts = place.parts
+    group = turned.shape[0]
+    many = wsum.shape[0] * (held // LANES)
+    lane = lax.broadcasted_iota(jnp.int32, (1, LANES), 1)
+    heavy = [jnp.where(lane < some, weights[src : src + 1, :], 0.0) for src in range(parts)]
+    tall = lax.broadcasted_iota(jnp.int32, (many, LANES), 0)
+    low = lax.broadcasted_iota(jnp.int32, (LANES, LANES), 0)
+    first = place.part * (many * LANES)
+
+    def weigh(m, total):
+        ones, loads = [], []
+        for src in range(parts):
+            spots = turned[m, src : src + 1, :] - first
+            loads.append(jnp.where((spots >> 7) == tall, heavy[src], 0.0).astype(jnp.bfloat16))
+            ones.append(jnp.where((spots & (LANES - 1)) == low, 1.0, 0.0).astype(jnp.bfloat16))
+        return total + lax.dot_general(
+            jnp.concatenate(loads, axis=1),
+            jnp.concatenate(ones, axis=1),
+            (((1,), (1,)), ((), ())),
+            preferred_element_type=jnp.float32,
+        )
+
+    total = lax.fori_loop(0, group, weigh, jnp.zeros((many, LANES), jnp.float32), unroll=True)
+    per = held // LANES
+    for b in range(wsum.shape[0]):
+        wsum[b, :per, :] = total[b * per : (b + 1) * per, :]
+        if per < SUBS:
+            wsum[b, per:, :] = jnp.zeros((SUBS - per, LANES), jnp.float32)
+
+
+def settle(place, some, turned, weights, acc, noisy, cube, out, wsum, got, sent, zgot, wgot, send, recv, wsend, wrecv, then=None):
     held = noisy.shape[0]
     collect = Collect(place, acc, got, sent, zgot, send, recv)
     place.greet()
+    weigh_rows(place, some, held, turned, weights, wsum)
+    place.meet()
     collect.begin()
     for d in range(1, place.ranks):
         collect.start(
@@ -507,6 +550,7 @@
     ranks = count // parts
     half = (parts, ranks // 2, held, LANES)
     return [
+        pltpu.VMEM((ranks, SUBS, LANES), jnp.float32),
         pltpu.VMEM((parts, ranks, held, LANES), dtype),
         pltpu.VMEM(half, dtype),
         pltpu.VMEM((parts, held, LANES), dtype),
@@ -518,7 +562,7 @@
     ]
 
 
-def second_kernel(count, some, acc, wsum, noisy, cube, cube_t, sigma, turned, same, coeffs_in, basic, back, weights, *scratch):
+def second_kernel(count, some, acc, weights_in, noisy, cube, cube_t, sigma, turned, same, coeffs_in, basic, back, weights, *scratch):
     stage, got, table, send, recv = scratch[:5]
     members, energy, ebuf, egot, esend, erecv = scratch[5:11]
     coeffs, csem, lsem = scratch[11:14]
@@ -531,15 +575,21 @@
     copies = to_scalars(turned, scalars, lsem)
     spread = Spread(place, stage, got, table, send, recv)
     ebuf[...] = jnp.zeros(ebuf.shape, ebuf.dtype)
+    def spread_piece(h):
+        spread.transform([h], basic, cube_t)
+        spread.begin([h])
+
     collect = settle(
         place,
+        some,
+        turned,
+        weights_in,
         acc,
-        wsum,
         noisy,
         cube,
         basic,
         *scratch[14 + group :],
-        then=lambda h: spread.begin([h], basic, cube_t),
+        then=spread_piece,
     )
     spread.finish()
     for copy in copies:
@@ -553,20 +603,19 @@
     spread.close()
 
 
-def third_kernel(count, parts, acc, wsum, noisy, cube, out, *scratch):
-    settle(Place(count, parts), acc, wsum, noisy, cube, out, *scratch).close()
-
-
-def add_kernel(count, some, carried, turned, weights, back, *refs):
+def third_kernel(count, parts, some, acc, weights, noisy, cube, turned, out, *scratch):
+    settle(Place(count, parts), some, turned, weights, acc, noisy, cube, out, *scratch).close()
+
+
+def add_kernel(some, carried, turned, weights, back, *refs):
     group, refs_here = back.shape[:2]
     parts = refs_here // some
     kept = refs[:carried]
-    acc, wsum = refs[carried : carried + 2]
-    outs = refs[carried + 2 : 2 * carried + 2]
-    members, ksem, lsem = refs[2 * carried + 2 : 2 * carried + 5]
-    scalars = refs[2 * carried + 5 : 2 * carried + 5 + group]
-    sums = refs[2 * carried + 5 + group :]
-    place = Place(count, parts)
+    acc = refs[carried]
+    outs = refs[carried + 1 : 2 * carried + 1]
+    heavy, ksem, lsem = refs[2 * carried + 1 : 2 * carried + 4]
+    scalars = refs[2 * carried + 4 : 2 * carried + 4 + group]
+    sums = refs[2 * carried + 4 + group :]
     blocks, held = acc.shape[:2]
     copies = to_scalars(turned, scalars, lsem)
     moves = [pltpu.make_async_copy(src, dst, ksem.at[i]) for i, (src, dst) in enumerate(zip(kept, outs))]
@@ -583,42 +632,7 @@
     for src in range(parts):
         row = jnp.broadcast_to(weights[src : src + 1, :], (some, LANES))
         column = jnp.sum(jnp.where(diagonal(some), row, 0.0), axis=1, keepdims=True)
-        spread = jnp.broadcast_to(column, (some, LANES))
-        rows = pl.ds(src * some, some)
-
-        def scale(m, carry):
-            members[m, rows, :] = back[m, rows, :].astype(jnp.float32) * spread
-            return carry
-
-        lax.fori_loop(0, group, scale, 0)
-
-    many = wsum.shape[0] * (held // LANES)
-    lane = lax.broadcasted_iota(jnp.int32, (1, LANES), 1)
-    heavy = [jnp.where(lane < some, weights[src : src + 1, :], 0.0) for src in range(parts)]
-    tall = lax.broadcasted_iota(jnp.int32, (many, LANES), 0)
-    low = lax.broadcasted_iota(jnp.int32, (LANES, LANES), 0)
-    first = place.part * (many * LANES)
-
-    def weigh(m, total):
-        ones, loads = [], []
-        for src in range(parts):
-            spots = turned[m, src : src + 1, :] - first
-            loads.append(jnp.where((spots >> 7) == tall, heavy[src], 0.0).astype(jnp.bfloat16))
-            ones.append(jnp.where((spots & (LANES - 1)) == low, 1.0, 0.0).astype(jnp.bfloat16))
-        return total + lax.dot_general(
-            jnp.concatenate(loads, axis=1),
-            jnp.concatenate(ones, axis=1),
-            (((1,), (1,)), ((), ())),
-            preferred_element_type=jnp.float32,
-        )
-
-    total = lax.fori_loop(0, group, weigh, jnp.zeros((many, LANES), jnp.float32), unroll=True)
-    per = held // LANES
-    for b in range(wsum.shape[0]):
-        wsum[b, :per, :] = total[b * per : (b + 1) * per, :]
-        if per < SUBS:
-            wsum[b, per:, :] = jnp.zeros((SUBS - per, LANES), jnp.float32)
-
+        heavy[src * some : (src + 1) * some, :] = jnp.broadcast_to(column, (some, LANES))
     together = group // STREAMS
     for copy in copies:
         copy.wait()
@@ -627,10 +641,12 @@
         src, row = t // (some // SUBS), lax.rem(t, some // SUBS)
         for q in range(SUBS):
             spots, news = [], []
+            weight = heavy[pl.ds(t * SUBS + q, 1), :]
             for m in range(group):
                 spot = scalars[m][src, row * SUBS + q]
                 spots.append(spot)
-                news.append(sums[m // together][pl.ds(spot, 1), :] + members[m, pl.ds(t * SUBS + q, 1), :])
+                each = weight * back[m, pl.ds(t * SUBS + q, 1), :]
+                news.append(sums[m // together][pl.ds(spot, 1), :] + each)
             for m in range(group):
                 sums[m // together][pl.ds(spots[m], 1), :] = news[m]
         return carry
@@ -662,16 +678,15 @@
     )
 
 
-def add_up(count, some, held, turned, weights, back, *kept):
+def add_up(count, some, held, dtype, turned, weights, back, *kept):
     group, refs = back.shape[:2]
-    ranks = count // (refs // some)
     return pl.pallas_call(
-        functools.partial(add_kernel, count, some, len(kept)),
-        out_shape=[shape(count, held, LANES, dtype=back.dtype), shape(ranks, SUBS, LANES)]
+        functools.partial(add_kernel, some, len(kept)),
+        out_shape=[shape(count, held, LANES, dtype=dtype)]
         + [shape(*each.shape, dtype=each.dtype) for each in kept],
         in_specs=[VMEM] * (3 + len(kept)),
-        out_specs=[VMEM, VMEM] + [HBM] * len(kept),
-        scratch_shapes=[pltpu.VMEM((group, refs, LANES), jnp.float32), SEMS((1,)), SEMS((group,))]
+        out_specs=[VMEM] + [HBM] * len(kept),
+        scratch_shapes=[pltpu.VMEM((refs, LANES), jnp.float32), SEMS((1,)), SEMS((group,))]
         + [pltpu.SMEM((SUBS, LANES), jnp.int32)] * group
         + [pltpu.VMEM((count * held, LANES), jnp.float32)] * STREAMS,
         compiler_params=params(count * held),
@@ -693,7 +708,7 @@
         functools.partial(first_kernel, count),
         out_shape=[
             shape(group, refs, LANES),
-            shape(group, refs, LANES, dtype=dtype),
+            shape(group, refs, LANES),
             shape(SUBS, LANES),
             shape(refs, LANES),
             shape(group, SUBS, LANES, dtype=jnp.int32),
@@ -720,12 +735,12 @@
         compiler_params=params(count * held, 0),
         name="shrink",
     )(*[pltpu.with_memory_space_constraint(v, pltpu.HBM) for v in (noisy, cube_home, matches.T, sigma, jnp.asarray(cube_t))])
-    acc, wsum = add_up(count, some, held, turned, weights, back)
+    (acc,) = add_up(count, some, held, dtype, turned, weights, back)
     basic, back, weights = pl.pallas_call(
         functools.partial(second_kernel, count, some),
         out_shape=[
             shape(held, width, dtype=dtype),
-            shape(group, refs, LANES, dtype=dtype),
+            shape(group, refs, LANES),
             shape(SUBS, LANES),
         ],
         in_specs=[VMEM] * 8 + [HBM],
@@ -736,17 +751,17 @@
         + settle_scratch(count, parts, held, dtype),
         compiler_params=params(count * held, 1),
         name="wiener",
-    )(acc, wsum, noisy, cube, cube_t, sigma, turned, same, coeffs)
-    acc, wsum, basic = add_up(count, some, held, turned, weights, back, basic)
+    )(acc, weights, noisy, cube, cube_t, sigma, turned, same, coeffs)
+    acc, basic = add_up(count, some, held, dtype, turned, weights, back, basic)
     final = pl.pallas_call(
-        functools.partial(third_kernel, count, parts),
+        functools.partial(third_kernel, count, parts, some),
         out_shape=shape(held, width, dtype=dtype),
-        in_specs=[VMEM] * 4,
+        in_specs=[VMEM] * 5,
         out_specs=VMEM,
         scratch_shapes=settle_scratch(count, parts, held, dtype),
         compiler_params=params(count * held, 2),
         name="settle",
-    )(acc, wsum, noisy, cube)
+    )(acc, weights, noisy, cube, turned)
     return basic, final
 
 

time: 122 us -> 123 us (level)
    pallas_call x1, Pallas kernels: 47.8 us -> 49.9 us  [body(): pl.pallas_call(functools.partial(second_kernel, count, some), out_shape=[...]
    pallas_call x3, Pallas kernels: 38 us -> 36 us  [the longest x1 20.9 us: body(): pl.pallas_call(functools.partial(third_kernel, count, parts, some), out_s...]
where the time goes in v6:
time: 123 us; the launch traced here: 122 us
  Pallas kernels  121 us (98%)
    pallas_call x1, Pallas kernels, body(): pl.pallas_call(functools.partial(second_kernel, count, some), out_shape=[...  49.9 us
    pallas_call x1, Pallas kernels, body(): pl.pallas_call(functools.partial(first_kernel, count), out_shape=[shape(g...  35 us
    pallas_call x1, Pallas kernels, body(): pl.pallas_call(functools.partial(third_kernel, count, parts, some), out_s...  20.9 us
    pallas_call x2, Pallas kernels, add_up(): pl.pallas_call(functools.partial(add_kernel, some, len(kept)), out_shape=...  15.1 us

profile of v6, /device:TPU:0, one launch (start us, length us, event | category | flops | bytes accessed | tf_op | source)
XLA Modules:
  0.0 122.5 jit_solution(11161920203995303121)
XLA Ops:
  0.6 0.0 copy-start
  0.6 0.0 copy-start.1
  0.7 0.0 copy-start.2
  0.7 0.0 copy-start.3
  0.7 35.0 %shrink.1 = (f32[16,384,128]{2,1,0:T(8,128)S(1)}, f32[16,384,128]{2,1,0:T(8,128)S(1)}, f32[8,128]{1,0:T(8,128)S(1)}, f32[384,128]{1,0:T(8,128)S(1)}, s32[16,8,128]{2,1,0:T(8,128)S(1)}) custom-call(bf16[512,512]{1,0:T(8,128)(2,1)} %noisy.3, s32[8192]{0:T(1024)} %home_in.1, s32[16,96]{1,0:T(8,128)} %bitcast.4, f32[1,512]{1,0:T(1,128)} %bitcast.2, ...), custom_call_target="tpu_custom_call" | custom-call | tf_op jit(solution)/shard_map/shrink/pallas_call | solution.py:707
  35.7 7.5 %add_up.2.acc = bf16[16,512,128]{2,1,0:T(8,128)(2,1)S(1)} custom-call(s32[16,8,128]{2,1,0:T(8,128)S(1)} %get-tuple-element.12.turned, f32[8,128]{1,0:T(8,128)S(1)} %get-tuple-element.13.weights.weights_in, f32[16,384,128]{2,1,0:T(8,128)S(1)} %get-tuple-element.14.back), custom_call_target="tpu_custom_call" | custom-call | tf_op jit(solution)/shard_map/add_up/pallas_call | solution.py:683
  43.3 0.0 copy-done
  43.3 0.0 copy-done.1
  43.3 0.0 copy-done.2
  43.3 0.0 copy-done.3
  43.3 49.9 %wiener.1 = (bf16[512,512]{1,0:T(8,128)(2,1)S(1)}, f32[16,384,128]{2,1,0:T(8,128)S(1)}, f32[8,128]{1,0:T(8,128)S(1)}) custom-call(bf16[16,512,128]{2,1,0:T(8,128)(2,1)S(1)} %add_up.2.acc, f32[8,128]{1,0:T(8,128)S(1)} %get-tuple-element.13.weights.weights_in, bf16[512,512]{1,0:T(8,128)(2,1)S(1)} %copy-done, bf16[512,512]{1,0:T(8,128)(2,1)S(1)} %copy-done.2, ...), custom_call_target="tpu_custom_call" | custom-call | tf_op jit(solution)/shard_map/wiener/pallas_call | solution.py:739
  93.2 7.5 %add_up.3 = (bf16[16,512,128]{2,1,0:T(8,128)(2,1)S(1)}, bf16[512,512]{1,0:T(8,128)(2,1)}) custom-call(s32[16,8,128]{2,1,0:T(8,128)S(1)} %get-tuple-element.12.turned, f32[8,128]{1,0:T(8,128)S(1)} %get-tuple-element.17.weights, f32[16,384,128]{2,1,0:T(8,128)S(1)} %get-tuple-element.18.back, bf16[512,512]{1,0:T(8,128)(2,1)S(1)} %get-tuple-element.19.refs_0_), custom_call_target="tpu_custom_call" | custom-call | tf_op jit(solution)/shard_map/add_up/pallas_call | solution.py:683
  100.7 20.9 %settle.1 = bf16[512,512]{1,0:T(8,128)(2,1)S(1)} custom-call(bf16[16,512,128]{2,1,0:T(8,128)(2,1)S(1)} %get-tuple-element.21.acc, f32[8,128]{1,0:T(8,128)S(1)} %get-tuple-element.17.weights, bf16[512,512]{1,0:T(8,128)(2,1)S(1)} %copy-done, bf16[512,512]{1,0:T(8,128)(2,1)S(1)} %copy-done.2, s32[16,8,128]{2,1,0:T(8,128)S(1)} %get-tuple-element.12.turned), custom_call_target="tpu_custom_call" | custom-call | tf_op jit(solution)/shard_map/settle/pallas_call | solution.py:756
  121.7 0.8 copy.9
Async XLA Ops:
  0.6 42.6 %copy-start = (bf16[512,512]{1,0:T(8,128)(2,1)S(1)}, bf16[512,512]{1,0:T(8,128)(2,1)}, u32[]{:S(2)}) copy-start(bf16[512,512]{1,0:T(8,128)(2,1)} %noisy.3) | copy-start | bytes 1572868
  0.6 42.6 %copy-start.1 = (bf16[512,512]{1,0:T(8,128)(2,1)S(1)}, bf16[512,512]{1,0:T(8,128)(2,1)}, u32[]{:S(2)}) copy-start(bf16[512,512]{1,0:T(8,128)(2,1)} %constant.4.clone.cube_in.cube_t) | copy-start | bytes 1572868
  0.7 42.6 %copy-start.2 = (bf16[512,512]{1,0:T(8,128)(2,1)S(1)}, bf16[512,512]{1,0:T(8,128)(2,1)}, u32[]{:S(2)}) copy-start(bf16[512,512]{1,0:T(8,128)(2,1)} %constant.5.clone.cube) | copy-start | bytes 1572868
  0.7 42.6 %copy-start.3 = (f32[512]{0:T(512)S(1)}, f32[512]{0:T(512)}, u32[]{:S(2)}) copy-start(f32[512]{0:T(512)} %param.9) | copy-start | bytes 6148

commit v7 on v6

--- a/solution.py
+++ b/solution.py
@@ -222,18 +222,12 @@
     ]
 
 
-def pick_rows(table, lists, members, some):
-    group = members.shape[0]
-
-    def step(t, carry):
-        src, row = t // (some // SUBS), lax.rem(t, some // SUBS)
-        for q in range(SUBS):
-            for m in range(group):
-                spot = lists[m][src, row * SUBS + q]
-                members[m, pl.ds(t * SUBS + q, 1), :] = table[pl.ds(spot, 1), :]
-        return carry
-
-    lax.fori_loop(0, members.shape[1] // SUBS, step, 0)
+def pick_rows(table, lists, t, some, picked):
+    src, row = t // (some // SUBS), lax.rem(t, some // SUBS)
+    for q in range(SUBS):
+        for m in range(picked.shape[0]):
+            spot = lists[m][src, row * SUBS + q]
+            picked[m, q : q + 1, :] = table[pl.ds(spot, 1), :]
 
 
 def to_scalars(lists, scalars, sem):
@@ -256,16 +250,16 @@
     return lax.broadcasted_iota(jnp.int32, shape, 0) == lax.broadcasted_iota(jnp.int32, shape, 1)
 
 
-def shrink_groups(place, second, width, some, sigma, members, coeffs, back, same, energy, ebuf, egot, weights, send, recv, then=None):
+def shrink_groups(place, second, width, some, table, lists, sigma, first, other, members, coeffs, back, same, energy, ebuf, egot, weights, send, recv, then=None):
     group, refs = members.shape[:2]
     factor = scales(group)
     columns = pl.ds(pl.multiple_of(place.part * LANES, LANES), LANES)
     own = sigma[:, columns]
     level = own * own if second else (shrink_level * own) * (shrink_level * own)
 
-    def forward(b, carry):
+    def forward(b, picked):
         rows = pl.ds(pl.multiple_of(b * SUBS, SUBS), SUBS)
-        values = cosine_sums([members[m, rows, :] for m in range(group)])
+        values = cosine_sums([picked[m] for m in range(group)])
         total = None
         for j in range(group):
             value = values[j] * factor[j]
@@ -279,9 +273,18 @@
                 coeffs[j, rows, :] = value
                 members[j, rows, :] = gain * value
         energy[rows, :] = total * level if second else total
+
+    blocks = refs // SUBS
+    pick_rows(table, lists, 0, some, first)
+
+    def pair(i, carry):
+        pick_rows(table, lists, 2 * i + 1, some, other)
+        forward(2 * i, first)
+        pick_rows(table, lists, jnp.minimum(2 * i + 2, blocks - 1), some, first)
+        forward(2 * i + 1, other)
         return carry
 
-    lax.fori_loop(0, refs // SUBS, forward, 0)
+    lax.fori_loop(0, blocks // 2, pair, 0)
     if then is not None:
         then()
     parts = refs // some
@@ -295,7 +298,7 @@
         started.append(copy)
 
     def inverse(b, carry):
-        rows = pl.ds(pl.multiple_of(b * SUBS, SUBS), SUBS)
+        rows = pl.ds(pl.multiple_of(b * 2 * SUBS, 2 * SUBS), 2 * SUBS)
         values = cosine_sums_transposed([members[j, rows, :] * factor[j] for j in range(group)])
         for m in range(group):
             merged = values[m]
@@ -305,7 +308,7 @@
             back[m, rows, :] = merged.astype(back.dtype)
         return carry
 
-    lax.fori_loop(0, refs // SUBS, inverse, 0)
+    lax.fori_loop(0, refs // (2 * SUBS), inverse, 0)
     total = ebuf[...]
     for off in range(1, place.parts):
         remote(ebuf, egot.at[off], send.at[off], recv.at[off], place.device(off, 0)).wait_recv()
@@ -318,6 +321,8 @@
 def shrink_scratch(parts, group, refs):
     assert parts <= SUBS
     return [
+        pltpu.VMEM((group, SUBS, LANES), jnp.float32),
+        pltpu.VMEM((group, SUBS, LANES), jnp.float32),
         pltpu.VMEM((group, refs, LANES), jnp.float32),
         pltpu.VMEM((refs, LANES), jnp.float32),
         pltpu.VMEM((SUBS, LANES), jnp.float32),
@@ -329,10 +334,10 @@
 
 def first_kernel(count, x_in, home_in, ids_in, sigma_in, cube_in, coeffs_out, back, weights, same, turned, *scratch):
     stage, got, table, send, recv = scratch[:5]
-    members, energy, ebuf, egot, esend, erecv = scratch[5:11]
-    x, cube_t, sigma, ids, insem = scratch[11:16]
-    coeffs, csem, home, named, lists_v, lsend, lrecv, lsem = scratch[16:24]
-    scalars = scratch[24:]
+    first, other, members, energy, ebuf, egot, esend, erecv = scratch[5:13]
+    x, cube_t, sigma, ids, insem = scratch[13:18]
+    coeffs, csem, home, named, lists_v, lsend, lrecv, lsem = scratch[18:26]
+    scalars = scratch[26:]
     parts = stage.shape[0]
     group, some = ids.shape
     place = Place(count, parts)
@@ -396,10 +401,9 @@
     spread.finish(lists_ready)
     for copy in copies:
         copy.wait()
-    pick_rows(table, scalars, members, some)
     store = pltpu.make_async_copy(coeffs, coeffs_out, csem.at[0])
     shrink_groups(
-        place, False, x.shape[1], some, sigma, members, coeffs, back, same, energy, ebuf, egot, weights, esend, erecv, store.start
+        place, False, x.shape[1], some, table, scalars, sigma, first, other, members, coeffs, back, same, energy, ebuf, egot, weights, esend, erecv, store.start
     )
     store.wait()
     for copy in started:
@@ -564,10 +568,10 @@
 
 def second_kernel(count, some, acc, weights_in, noisy, cube, cube_t, sigma, turned, same, coeffs_in, basic, back, weights, *scratch):
     stage, got, table, send, recv = scratch[:5]
-    members, energy, ebuf, egot, esend, erecv = scratch[5:11]
-    coeffs, csem, lsem = scratch[11:14]
+    first, other, members, energy, ebuf, egot, esend, erecv = scratch[5:13]
+    coeffs, csem, lsem = scratch[13:16]
     group = members.shape[0]
-    scalars = scratch[14 : 14 + group]
+    scalars = scratch[16 : 16 + group]
     parts = stage.shape[0]
     place = Place(count, parts)
     fetch = pltpu.make_async_copy(coeffs_in, coeffs, csem.at[0])
@@ -588,16 +592,15 @@
         noisy,
         cube,
         basic,
-        *scratch[14 + group :],
+        *scratch[16 + group :],
         then=spread_piece,
     )
     spread.finish()
     for copy in copies:
         copy.wait()
-    pick_rows(table, scalars, members, some)
     fetch.wait()
     shrink_groups(
-        place, True, noisy.shape[1], some, sigma, members, coeffs, back, same, energy, ebuf, egot, weights, esend, erecv
+        place, True, noisy.shape[1], some, table, scalars, sigma, first, other, members, coeffs, back, same, energy, ebuf, egot, weights, esend, erecv
     )
     collect.close()
     spread.close()

time: 123 us -> 116 us (0.943)
  Pallas kernels: 121 us -> 114 us
    pallas_call x1, Pallas kernels: 49.9 us -> 45.9 us  [body(): pl.pallas_call(functools.partial(second_kernel, count, some), out_shape=[...]
    pallas_call x1, Pallas kernels: 35 us -> 31.8 us  [body(): pl.pallas_call(functools.partial(first_kernel, count), out_shape=[shape(g...]
where the time goes in v7:
time: 116 us; the launch traced here: 115 us
  Pallas kernels  114 us (98%)
    pallas_call x1, Pallas kernels, body(): pl.pallas_call(functools.partial(second_kernel, count, some), out_shape=[...  45.9 us
    pallas_call x1, Pallas kernels, body(): pl.pallas_call(functools.partial(first_kernel, count), out_shape=[shape(g...  31.8 us
    pallas_call x1, Pallas kernels, body(): pl.pallas_call(functools.partial(third_kernel, count, parts, some), out_s...  21 us
    pallas_call x2, Pallas kernels, add_up(): pl.pallas_call(functools.partial(add_kernel, some, len(kept)), out_shape=...  15.1 us

profile of v7, /device:TPU:0, one launch (start us, length us, event | category | flops | bytes accessed | tf_op | source)
XLA Modules:
  0.0 115.4 jit_solution(8234810515678014376)
XLA Ops:
  0.6 0.0 copy-start
  0.6 0.0 copy-start.1
  0.7 0.0 copy-start.2
  0.7 0.0 copy-start.3
  0.7 31.8 %shrink.1 = (f32[16,384,128]{2,1,0:T(8,128)S(1)}, f32[16,384,128]{2,1,0:T(8,128)S(1)}, f32[8,128]{1,0:T(8,128)S(1)}, f32[384,128]{1,0:T(8,128)S(1)}, s32[16,8,128]{2,1,0:T(8,128)S(1)}) custom-call(bf16[512,512]{1,0:T(8,128)(2,1)} %noisy.3, s32[8192]{0:T(1024)} %home_in.1, s32[16,96]{1,0:T(8,128)} %bitcast.4, f32[1,512]{1,0:T(1,128)} %bitcast.2, ...), custom_call_target="tpu_custom_call" | custom-call | tf_op jit(solution)/shard_map/shrink/pallas_call | solution.py:710
  32.5 7.5 %add_up.2.acc = bf16[16,512,128]{2,1,0:T(8,128)(2,1)S(1)} custom-call(s32[16,8,128]{2,1,0:T(8,128)S(1)} %get-tuple-element.12.turned, f32[8,128]{1,0:T(8,128)S(1)} %get-tuple-element.13.weights.weights_in, f32[16,384,128]{2,1,0:T(8,128)S(1)} %get-tuple-element.14.back), custom_call_target="tpu_custom_call" | custom-call | tf_op jit(solution)/shard_map/add_up/pallas_call | solution.py:686
  40.1 0.0 copy-done
  40.1 0.0 copy-done.1
  40.1 0.0 copy-done.2
  40.1 0.0 copy-done.3
  40.1 45.9 %wiener.1 = (bf16[512,512]{1,0:T(8,128)(2,1)S(1)}, f32[16,384,128]{2,1,0:T(8,128)S(1)}, f32[8,128]{1,0:T(8,128)S(1)}) custom-call(bf16[16,512,128]{2,1,0:T(8,128)(2,1)S(1)} %add_up.2.acc, f32[8,128]{1,0:T(8,128)S(1)} %get-tuple-element.13.weights.weights_in, bf16[512,512]{1,0:T(8,128)(2,1)S(1)} %copy-done, bf16[512,512]{1,0:T(8,128)(2,1)S(1)} %copy-done.2, ...), custom_call_target="tpu_custom_call" | custom-call | tf_op jit(solution)/shard_map/wiener/pallas_call | solution.py:742
  86.0 7.5 %add_up.3 = (bf16[16,512,128]{2,1,0:T(8,128)(2,1)S(1)}, bf16[512,512]{1,0:T(8,128)(2,1)}) custom-call(s32[16,8,128]{2,1,0:T(8,128)S(1)} %get-tuple-element.12.turned, f32[8,128]{1,0:T(8,128)S(1)} %get-tuple-element.17.weights, f32[16,384,128]{2,1,0:T(8,128)S(1)} %get-tuple-element.18.back, bf16[512,512]{1,0:T(8,128)(2,1)S(1)} %get-tuple-element.19.refs_0_), custom_call_target="tpu_custom_call" | custom-call | tf_op jit(solution)/shard_map/add_up/pallas_call | solution.py:686
  93.6 21.0 %settle.1 = bf16[512,512]{1,0:T(8,128)(2,1)S(1)} custom-call(bf16[16,512,128]{2,1,0:T(8,128)(2,1)S(1)} %get-tuple-element.21.acc, f32[8,128]{1,0:T(8,128)S(1)} %get-tuple-element.17.weights, bf16[512,512]{1,0:T(8,128)(2,1)S(1)} %copy-done, bf16[512,512]{1,0:T(8,128)(2,1)S(1)} %copy-done.2, s32[16,8,128]{2,1,0:T(8,128)S(1)} %get-tuple-element.12.turned), custom_call_target="tpu_custom_call" | custom-call | tf_op jit(solution)/shard_map/settle/pallas_call | solution.py:759
  114.6 0.8 copy.9
Async XLA Ops:
  0.6 39.4 %copy-start = (bf16[512,512]{1,0:T(8,128)(2,1)S(1)}, bf16[512,512]{1,0:T(8,128)(2,1)}, u32[]{:S(2)}) copy-start(bf16[512,512]{1,0:T(8,128)(2,1)} %noisy.3) | copy-start | bytes 1572868
  0.6 39.4 %copy-start.1 = (bf16[512,512]{1,0:T(8,128)(2,1)S(1)}, bf16[512,512]{1,0:T(8,128)(2,1)}, u32[]{:S(2)}) copy-start(bf16[512,512]{1,0:T(8,128)(2,1)} %constant.4.clone.cube_in.cube_t) | copy-start | bytes 1572868
  0.7 39.4 %copy-start.2 = (bf16[512,512]{1,0:T(8,128)(2,1)S(1)}, bf16[512,512]{1,0:T(8,128)(2,1)}, u32[]{:S(2)}) copy-start(bf16[512,512]{1,0:T(8,128)(2,1)} %constant.5.clone.cube) | copy-start | bytes 1572868
  0.7 39.4 %copy-start.3 = (f32[512]{0:T(512)S(1)}, f32[512]{0:T(512)}, u32[]{:S(2)}) copy-start(f32[512]{0:T(512)} %param.9) | copy-start | bytes 6148

commit v8 on v7

--- a/solution.py
+++ b/solution.py
@@ -284,7 +284,7 @@
         forward(2 * i + 1, other)
         return carry
 
-    lax.fori_loop(0, blocks // 2, pair, 0)
+    lax.fori_loop(0, blocks // 2, pair, 0, unroll=2)
     if then is not None:
         then()
     parts = refs // some
@@ -415,7 +415,7 @@
     def __init__(self, place, acc, got, sent, zgot, send, recv):
         self.place, self.acc, self.got, self.sent, self.zgot = place, acc, got, sent, zgot
         self.send, self.recv, self.started = send, recv, []
-        self.order = list(range(place.parts - 1, -1, -1))
+        self.order = sorted(range(1, place.parts), key=lambda off: (off % 2, off)) + [0]
 
     def start(self, copy):
         copy.start()

time: 116 us -> 114 us (0.983)
  Pallas kernels: 114 us -> 112 us
where the time goes in v8:
time: 114 us
  Pallas kernels  112 us (98%)
    pallas_call x1, Pallas kernels, body(): pl.pallas_call(functools.partial(second_kernel, count, some), out_shape=[...  45.2 us
    pallas_call x1, Pallas kernels, body(): pl.pallas_call(functools.partial(first_kernel, count), out_shape=[shape(g...  31.6 us
    pallas_call x1, Pallas kernels, body(): pl.pallas_call(functools.partial(third_kernel, count, parts, some), out_s...  20.5 us
    pallas_call x2, Pallas kernels, add_up(): pl.pallas_call(functools.partial(add_kernel, some, len(kept)), out_shape=...  15.1 us

profile of v8, /device:TPU:0, one launch (start us, length us, event | category | flops | bytes accessed | tf_op | source)
XLA Modules:
  0.0 113.9 jit_solution(878973898773110560)
XLA Ops:
  0.6 0.0 copy-start
  0.6 0.0 copy-start.1
  0.7 0.0 copy-start.2
  0.7 0.0 copy-start.3
  0.7 31.6 %shrink.1 = (f32[16,384,128]{2,1,0:T(8,128)S(1)}, f32[16,384,128]{2,1,0:T(8,128)S(1)}, f32[8,128]{1,0:T(8,128)S(1)}, f32[384,128]{1,0:T(8,128)S(1)}, s32[16,8,128]{2,1,0:T(8,128)S(1)}) custom-call(bf16[512,512]{1,0:T(8,128)(2,1)} %noisy.3, s32[8192]{0:T(1024)} %home_in.1, s32[16,96]{1,0:T(8,128)} %bitcast.4, f32[1,512]{1,0:T(1,128)} %bitcast.2, ...), custom_call_target="tpu_custom_call" | custom-call | tf_op jit(solution)/shard_map/shrink/pallas_call | solution.py:710
  32.2 7.5 %add_up.2.acc = bf16[16,512,128]{2,1,0:T(8,128)(2,1)S(1)} custom-call(s32[16,8,128]{2,1,0:T(8,128)S(1)} %get-tuple-element.12.turned, f32[8,128]{1,0:T(8,128)S(1)} %get-tuple-element.13.weights.weights_in, f32[16,384,128]{2,1,0:T(8,128)S(1)} %get-tuple-element.14.back), custom_call_target="tpu_custom_call" | custom-call | tf_op jit(solution)/shard_map/add_up/pallas_call | solution.py:686
  39.8 0.0 copy-done
  39.8 0.0 copy-done.1
  39.8 0.0 copy-done.2
  39.8 0.0 copy-done.3
  39.8 45.2 %wiener.1 = (bf16[512,512]{1,0:T(8,128)(2,1)S(1)}, f32[16,384,128]{2,1,0:T(8,128)S(1)}, f32[8,128]{1,0:T(8,128)S(1)}) custom-call(bf16[16,512,128]{2,1,0:T(8,128)(2,1)S(1)} %add_up.2.acc, f32[8,128]{1,0:T(8,128)S(1)} %get-tuple-element.13.weights.weights_in, bf16[512,512]{1,0:T(8,128)(2,1)S(1)} %copy-done, bf16[512,512]{1,0:T(8,128)(2,1)S(1)} %copy-done.2, ...), custom_call_target="tpu_custom_call" | custom-call | tf_op jit(solution)/shard_map/wiener/pallas_call | solution.py:742
  85.1 7.5 %add_up.3 = (bf16[16,512,128]{2,1,0:T(8,128)(2,1)S(1)}, bf16[512,512]{1,0:T(8,128)(2,1)}) custom-call(s32[16,8,128]{2,1,0:T(8,128)S(1)} %get-tuple-element.12.turned, f32[8,128]{1,0:T(8,128)S(1)} %get-tuple-element.17.weights, f32[16,384,128]{2,1,0:T(8,128)S(1)} %get-tuple-element.18.back, bf16[512,512]{1,0:T(8,128)(2,1)S(1)} %get-tuple-element.19.refs_0_), custom_call_target="tpu_custom_call" | custom-call | tf_op jit(solution)/shard_map/add_up/pallas_call | solution.py:686
  92.6 20.5 %settle.1 = bf16[512,512]{1,0:T(8,128)(2,1)S(1)} custom-call(bf16[16,512,128]{2,1,0:T(8,128)(2,1)S(1)} %get-tuple-element.21.acc, f32[8,128]{1,0:T(8,128)S(1)} %get-tuple-element.17.weights, bf16[512,512]{1,0:T(8,128)(2,1)S(1)} %copy-done, bf16[512,512]{1,0:T(8,128)(2,1)S(1)} %copy-done.2, s32[16,8,128]{2,1,0:T(8,128)S(1)} %get-tuple-element.12.turned), custom_call_target="tpu_custom_call" | custom-call | tf_op jit(solution)/shard_map/settle/pallas_call | solution.py:759
  113.1 0.8 copy.9
Async XLA Ops:
  0.6 39.2 %copy-start = (bf16[512,512]{1,0:T(8,128)(2,1)S(1)}, bf16[512,512]{1,0:T(8,128)(2,1)}, u32[]{:S(2)}) copy-start(bf16[512,512]{1,0:T(8,128)(2,1)} %noisy.3) | copy-start | bytes 1572868
  0.6 39.2 %copy-start.1 = (bf16[512,512]{1,0:T(8,128)(2,1)S(1)}, bf16[512,512]{1,0:T(8,128)(2,1)}, u32[]{:S(2)}) copy-start(bf16[512,512]{1,0:T(8,128)(2,1)} %constant.4.clone.cube_in.cube_t) | copy-start | bytes 1572868
  0.7 39.2 %copy-start.2 = (bf16[512,512]{1,0:T(8,128)(2,1)S(1)}, bf16[512,512]{1,0:T(8,128)(2,1)}, u32[]{:S(2)}) copy-start(bf16[512,512]{1,0:T(8,128)(2,1)} %constant.5.clone.cube) | copy-start | bytes 1572868
  0.7 39.2 %copy-start.3 = (f32[512]{0:T(512)S(1)}, f32[512]{0:T(512)}, u32[]{:S(2)}) copy-start(f32[512]{0:T(512)} %param.9) | copy-start | bytes 6148

commit v9 on v8

--- a/solution.py
+++ b/solution.py
@@ -147,7 +147,7 @@
                 self.started.append(copy)
 
     def orders(self, hs):
-        return itertools.product(list(range(1, self.place.parts)) + [0], hs)
+        return itertools.product(range(self.place.parts), hs)
 
     def transform(self, hs, rows, cube_t):
         size = rows.shape[0] // PIECES

time: 114 us -> 114 us (level)
  no operation moved by 1% of the time
where the time goes in v9:
time: 114 us
  Pallas kernels  112 us (98%)
    pallas_call x1, Pallas kernels, body(): pl.pallas_call(functools.partial(second_kernel, count, some), out_shape=[...  45.2 us
    pallas_call x1, Pallas kernels, body(): pl.pallas_call(functools.partial(first_kernel, count), out_shape=[shape(g...  31.6 us
    pallas_call x1, Pallas kernels, body(): pl.pallas_call(functools.partial(third_kernel, count, parts, some), out_s...  20.5 us
    pallas_call x2, Pallas kernels, add_up(): pl.pallas_call(functools.partial(add_kernel, some, len(kept)), out_shape=...  15.1 us

profile of v9, /device:TPU:0, one launch (start us, length us, event | category | flops | bytes accessed | tf_op | source)
XLA Modules:
  0.0 113.9 jit_solution(4476337068104314841)
XLA Ops:
  0.6 0.0 copy-start
  0.6 0.0 copy-start.1
  0.7 0.0 copy-start.2
  0.7 0.0 copy-start.3
  0.7 31.6 %shrink.1 = (f32[16,384,128]{2,1,0:T(8,128)S(1)}, f32[16,384,128]{2,1,0:T(8,128)S(1)}, f32[8,128]{1,0:T(8,128)S(1)}, f32[384,128]{1,0:T(8,128)S(1)}, s32[16,8,128]{2,1,0:T(8,128)S(1)}) custom-call(bf16[512,512]{1,0:T(8,128)(2,1)} %noisy.3, s32[8192]{0:T(1024)} %home_in.1, s32[16,96]{1,0:T(8,128)} %bitcast.4, f32[1,512]{1,0:T(1,128)} %bitcast.2, ...), custom_call_target="tpu_custom_call" | custom-call | tf_op jit(solution)/shard_map/shrink/pallas_call | solution.py:710
  32.3 7.5 %add_up.2.acc = bf16[16,512,128]{2,1,0:T(8,128)(2,1)S(1)} custom-call(s32[16,8,128]{2,1,0:T(8,128)S(1)} %get-tuple-element.12.turned, f32[8,128]{1,0:T(8,128)S(1)} %get-tuple-element.13.weights.weights_in, f32[16,384,128]{2,1,0:T(8,128)S(1)} %get-tuple-element.14.back), custom_call_target="tpu_custom_call" | custom-call | tf_op jit(solution)/shard_map/add_up/pallas_call | solution.py:686
  39.8 0.0 copy-done
  39.8 0.0 copy-done.1
  39.8 0.0 copy-done.2
  39.8 0.0 copy-done.3
  39.8 45.2 %wiener.1 = (bf16[512,512]{1,0:T(8,128)(2,1)S(1)}, f32[16,384,128]{2,1,0:T(8,128)S(1)}, f32[8,128]{1,0:T(8,128)S(1)}) custom-call(bf16[16,512,128]{2,1,0:T(8,128)(2,1)S(1)} %add_up.2.acc, f32[8,128]{1,0:T(8,128)S(1)} %get-tuple-element.13.weights.weights_in, bf16[512,512]{1,0:T(8,128)(2,1)S(1)} %copy-done, bf16[512,512]{1,0:T(8,128)(2,1)S(1)} %copy-done.2, ...), custom_call_target="tpu_custom_call" | custom-call | tf_op jit(solution)/shard_map/wiener/pallas_call | solution.py:742
  85.1 7.5 %add_up.3 = (bf16[16,512,128]{2,1,0:T(8,128)(2,1)S(1)}, bf16[512,512]{1,0:T(8,128)(2,1)}) custom-call(s32[16,8,128]{2,1,0:T(8,128)S(1)} %get-tuple-element.12.turned, f32[8,128]{1,0:T(8,128)S(1)} %get-tuple-element.17.weights, f32[16,384,128]{2,1,0:T(8,128)S(1)} %get-tuple-element.18.back, bf16[512,512]{1,0:T(8,128)(2,1)S(1)} %get-tuple-element.19.refs_0_), custom_call_target="tpu_custom_call" | custom-call | tf_op jit(solution)/shard_map/add_up/pallas_call | solution.py:686
  92.6 20.5 %settle.1 = bf16[512,512]{1,0:T(8,128)(2,1)S(1)} custom-call(bf16[16,512,128]{2,1,0:T(8,128)(2,1)S(1)} %get-tuple-element.21.acc, f32[8,128]{1,0:T(8,128)S(1)} %get-tuple-element.17.weights, bf16[512,512]{1,0:T(8,128)(2,1)S(1)} %copy-done, bf16[512,512]{1,0:T(8,128)(2,1)S(1)} %copy-done.2, s32[16,8,128]{2,1,0:T(8,128)S(1)} %get-tuple-element.12.turned), custom_call_target="tpu_custom_call" | custom-call | tf_op jit(solution)/shard_map/settle/pallas_call | solution.py:759
  113.1 0.8 copy.9
Async XLA Ops:
  0.6 39.2 %copy-start = (bf16[512,512]{1,0:T(8,128)(2,1)S(1)}, bf16[512,512]{1,0:T(8,128)(2,1)}, u32[]{:S(2)}) copy-start(bf16[512,512]{1,0:T(8,128)(2,1)} %noisy.3) | copy-start | bytes 1572868
  0.6 39.2 %copy-start.1 = (bf16[512,512]{1,0:T(8,128)(2,1)S(1)}, bf16[512,512]{1,0:T(8,128)(2,1)}, u32[]{:S(2)}) copy-start(bf16[512,512]{1,0:T(8,128)(2,1)} %constant.4.clone.cube_in.cube_t) | copy-start | bytes 1572868
  0.7 39.2 %copy-start.2 = (bf16[512,512]{1,0:T(8,128)(2,1)S(1)}, bf16[512,512]{1,0:T(8,128)(2,1)}, u32[]{:S(2)}) copy-start(bf16[512,512]{1,0:T(8,128)(2,1)} %constant.5.clone.cube) | copy-start | bytes 1572868
  0.7 39.2 %copy-start.3 = (f32[512]{0:T(512)S(1)}, f32[512]{0:T(512)}, u32[]{:S(2)}) copy-start(f32[512]{0:T(512)} %param.9) | copy-start | bytes 6148
